TPU v7x, 512 devices: a whole 4x8x8 slice. The times are simulated.
512 devices in a mesh: dp: 2 (over y_hi), gx: 32 (over x, z), gy: 8 (over y_lo, core).
Axes of the slice: x: 4, y: 8 (y_hi: 2, y_lo: 4; y = y_hi * 4 + y_lo), z: 8, core: 2. Of those that a mesh axis runs over, the one named last changes fastest.
Arguments:
- fields: bfloat16 [2, 16, 256, 32768], P('dp', None, 'gx', 'gy'), may hold values from -6 to 6
- pre_act: bfloat16 [2, 16, 256, 32768], P('dp', None, 'gx', 'gy'), may hold values from -6 to 6
- cotangent: bfloat16 [2, 16, 256, 32768], P('dp', None, 'gx', 'gy'), may hold values from -6 to 6
- spec_weight: bfloat16 [2, 32, 32, 16, 256], P(None, 'gx', None, 'gy'), may hold values from -12 to 12
- point_weight: bfloat16 [16, 16], replicated, may hold values from -1.5 to 1.5
Outputs:
- grad_fields: bfloat16 [2, 16, 256, 32768], P('dp', None, 'gx', 'gy')
- grad_spec: float32 [2, 32, 32, 16, 256], P(None, 'gx', None, 'gy')
All inputs are finite; a program needn't handle non-finite values.
Results may differ from a plain program's by a relative error of at most 0.0098.
Values may be sent and summed in bfloat16 or wider, within the bound.
No kernel may reach another device: no remote copies, remote signals or barrier semaphores. Data moves between devices by JAX's collectives and lax.ppermute only.
A program may use at most 64 MiB of HBM per device.

v0:
```python
import math

import jax
import jax.numpy as jnp
from jax import lax
from jax.sharding import PartitionSpec as P

C = 16
NX = 256
NY = 512
NZ = 64
MX = 32
MY = 32
MZ = 16


def kept_freqs(kept, length, both_signs):
    index = jnp.arange(kept, dtype=jnp.int32)
    if both_signs:
        return jnp.where(index < kept // 2, index, length - kept + index)
    return index


def phase(freqs, points, length):
    turns = points[:, None] * freqs[None, :] % length
    return turns.astype(jnp.float32) * (2.0 * math.pi / length)


def forward_table(kept, length):
    angle = phase(kept_freqs(kept, length, True), jnp.arange(length, dtype=jnp.int32), length)
    cosine = jnp.cos(angle)
    minus_sine = -jnp.sin(angle)
    upper = jnp.stack([cosine, minus_sine], axis=-1)
    lower = jnp.stack([-minus_sine, cosine], axis=-1)
    return jnp.stack([upper, lower], axis=1).astype(jnp.bfloat16)


def inverse_table(kept, length, positions):
    angle = phase(kept_freqs(kept, length, True), positions, length)
    cosine = jnp.transpose(jnp.cos(angle))
    sine = jnp.transpose(jnp.sin(angle))
    upper = jnp.stack([cosine, sine], axis=-1)
    lower = jnp.stack([-sine, cosine], axis=-1)
    return jnp.stack([upper, lower], axis=1).astype(jnp.bfloat16)


def z_forward_table():
    angle = phase(kept_freqs(MZ, NZ, False), jnp.arange(NZ, dtype=jnp.int32), NZ)
    return (
        jnp.stack([jnp.cos(angle), -jnp.sin(angle)], axis=-1)
        .reshape(NZ, 2 * MZ)
        .astype(jnp.bfloat16)
    )


def z_inverse_table():
    angle = jnp.transpose(phase(kept_freqs(MZ, NZ, False), jnp.arange(NZ, dtype=jnp.int32), NZ))
    return (
        jnp.stack([jnp.cos(angle), -jnp.sin(angle)], axis=1)
        .reshape(2 * MZ, NZ)
        .astype(jnp.bfloat16)
    )


def gelu_slope(value):
    cdf = 0.5 * (1.0 + jax.scipy.special.erf(value * (1.0 / math.sqrt(2.0))))
    return cdf + value * jnp.exp(-0.5 * value * value) * (1.0 / math.sqrt(2.0 * math.pi))


def scale_modes(mode_values, weight_z):
    return mode_values.astype(jnp.float32) * weight_z[:, None]


def weight_grads(field_hat, grad_scaled):
    highest = lax.Precision.HIGHEST
    real_u = field_hat[..., 0].astype(jnp.float32)
    imag_u = field_hat[..., 1].astype(jnp.float32)
    real_d = grad_scaled[..., 0]
    imag_d = grad_scaled[..., 1]
    form = "bixyz,boxyz->xyzio"
    real_w = jnp.einsum(form, real_u, real_d, precision=highest) + jnp.einsum(
        form, imag_u, imag_d, precision=highest
    )
    imag_w = jnp.einsum(form, real_u, imag_d, precision=highest) - jnp.einsum(
        form, imag_u, real_d, precision=highest
    )
    result = jnp.stack([real_w, imag_w], axis=0)
    return result.reshape(result.shape[:4] + (C * C,))


def input_grads(spec_weight, grad_scaled):
    highest = lax.Precision.HIGHEST
    weights = spec_weight.astype(jnp.float32).reshape(spec_weight.shape[:4] + (C, C))
    real_d = grad_scaled[..., 0]
    imag_d = grad_scaled[..., 1]
    form = "xyzio,boxyz->bixyz"
    real_g = jnp.einsum(form, weights[0], real_d, precision=highest) + jnp.einsum(
        form, weights[1], imag_d, precision=highest
    )
    imag_g = jnp.einsum(form, weights[0], imag_d, precision=highest) - jnp.einsum(
        form, weights[1], real_d, precision=highest
    )
    return jnp.stack([real_g, imag_g], axis=-1).astype(jnp.bfloat16)


def on_device(fields, pre_act, cotangent, spec_weight, point_weight):
    count_x = lax.axis_size("gx")
    count_y = lax.axis_size("gy")
    local_batch, channels, local_x, local_yz = fields.shape
    local_y = local_yz // NZ
    sub_y = local_y // count_x
    local_mx = spec_weight.shape[1]
    local_mz = spec_weight.shape[3]
    stack_rows = 2 * local_batch * channels
    half_rows = local_batch * channels
    grad_pre = (cotangent.astype(jnp.float32) * gelu_slope(pre_act.astype(jnp.float32))).astype(
        jnp.bfloat16
    )
    stacked = jnp.concatenate([fields, grad_pre], axis=0)
    z_forward = z_forward_table()
    arrived = lax.all_to_all(
        stacked.reshape(stack_rows, local_x, local_yz),
        "gx",
        split_axis=2,
        concat_axis=1,
        tiled=True,
    )
    z_spectra = jnp.dot(
        arrived.reshape(stack_rows, NX, sub_y, NZ), z_forward, preferred_element_type=jnp.float32
    ).astype(jnp.bfloat16)
    z_spectra = z_spectra.reshape(stack_rows, NX, sub_y, MZ, 2)
    x_spectra = jnp.einsum(
        "sxyzr,xrkq->skyzq", z_spectra, forward_table(MX, NX), preferred_element_type=jnp.float32
    ).astype(jnp.bfloat16)
    x_spectra = x_spectra.reshape(stack_rows, MX, sub_y, 2 * MZ)
    mode_lines = lax.all_to_all(
        lax.all_to_all(x_spectra, "gx", split_axis=1, concat_axis=2, tiled=True),
        "gy",
        split_axis=3,
        concat_axis=2,
        tiled=True,
    )
    mode_lines = mode_lines.reshape(stack_rows, local_mx, NY, local_mz, 2)
    spectrum = jnp.einsum(
        "skyzr,yrlq->sklzq", mode_lines, forward_table(MY, NY), preferred_element_type=jnp.float32
    ).astype(jnp.bfloat16)
    spectrum = spectrum.reshape(2, local_batch, channels, local_mx, MY, local_mz, 2)
    field_hat = spectrum[0]
    grad_hat_in = spectrum[1]
    kz_index = lax.axis_index("gy") * local_mz + jnp.arange(local_mz, dtype=jnp.int32)
    weight_z = jnp.where(kz_index == 0, 1.0, 2.0).astype(jnp.float32) / float(NX * NY * NZ)
    grad_scaled = scale_modes(grad_hat_in, weight_z)
    grad_spec = lax.psum(weight_grads(field_hat, grad_scaled).astype(jnp.bfloat16), "dp").astype(
        jnp.float32
    )
    grad_hat = input_grads(spec_weight, grad_scaled).reshape(half_rows, local_mx, MY, local_mz, 2)
    span = count_y * sub_y
    order = jnp.arange(NY, dtype=jnp.int32)
    block = order // span
    rest = order % span
    positions = rest // sub_y * local_y + block * sub_y + rest % sub_y
    back_y = jnp.einsum(
        "sklzr,lryq->skyzq",
        grad_hat,
        inverse_table(MY, NY, positions),
        preferred_element_type=jnp.float32,
    ).astype(jnp.bfloat16)
    back_y = back_y.reshape(half_rows, local_mx, NY, 2 * local_mz)
    spread = lax.all_to_all(
        lax.all_to_all(back_y, "gx", split_axis=2, concat_axis=1, tiled=True),
        "gy",
        split_axis=2,
        concat_axis=3,
        tiled=True,
    )
    spread = spread.reshape(half_rows, MX, sub_y, MZ, 2)
    back_x = jnp.einsum(
        "skyzr,krxq->sxyzq",
        spread,
        inverse_table(MX, NX, jnp.arange(NX, dtype=jnp.int32)),
        preferred_element_type=jnp.float32,
    ).astype(jnp.bfloat16)
    returned = lax.all_to_all(
        back_x.reshape(half_rows, NX, sub_y * 2 * MZ), "gx", split_axis=1, concat_axis=2, tiled=True
    )
    spectral = jnp.dot(
        returned.reshape(half_rows, local_x, local_y, 2 * MZ),
        z_inverse_table(),
        preferred_element_type=jnp.float32,
    )
    spectral = spectral.reshape(local_batch, channels, local_x, local_yz)
    pointwise = jnp.einsum(
        "io,boxq->bixq", point_weight, grad_pre, preferred_element_type=jnp.float32
    )
    grad_fields = (spectral + pointwise).astype(jnp.bfloat16)
    return (grad_fields, grad_spec)


def solution(mesh):
    placed = (
        P("dp", None, "gx", "gy"),
        P("dp", None, "gx", "gy"),
        P("dp", None, "gx", "gy"),
        P(None, "gx", None, "gy", None),
        P(),
    )
    return jax.shard_map(
        on_device,
        mesh=mesh,
        in_specs=placed,
        out_specs=(P("dp", None, "gx", "gy"), P(None, "gx", None, "gy", None)),
        check_vma=False,
    )
```

profile of v0, /device:TPU:1, one launch (start us, length us, event | category | flops | bytes accessed | tf_op | source)
XLA Modules:
  0.0 255.6 jit_solution(6188466090925207576)
XLA Ops:
  7.2 2.3 fusion.11
  9.7 8.1 %copy.200 = bf16[32,8,4096]{0,1,2:T(8,128)(2,1)} copy(bf16[32,8,4096]{2,1,0:T(8,128)(2,1)S(1)} %bitcast.226) | data formatting | bytes 4194304 | tf_op jit(solution)/shard_map/reshape | solution.py:122
  17.8 13.3 %reshape.1022 = bf16[32,2,16384]{2,1,0:T(2,128)(2,1)} reshape(bf16[4096,8,32]{2,1,0:T(8,128)(2,1)} %bitcast.223) | data formatting | bytes 4194304
  31.1 13.8 %all-to-all-start = ((bf16[32,2,16384]{2,1,0:T(2,128)(2,1)}), bf16[32,2,16384]{2,1,0:T(2,128)(2,1)S(1)}, u32[]{:S(2)}, u32[]{:S(2)}) async-start(bf16[32,2,16384]{2,1,0:T(2,128)(2,1)} %reshape.1022), calls=%async_computation | async-start | bytes 4194304 | tf_op jit(solution)/shard_map/all_to_all | solution.py:121
  45.4 0.3 negate_convert_fusion
  45.7 48.1 %all-to-all-done = bf16[32,2,16384]{2,1,0:T(2,128)(2,1)S(1)} async-done(((bf16[32,2,16384]{2,1,0:T(2,128)(2,1)}), bf16[32,2,16384]{2,1,0:T(2,128)(2,1)S(1)}, u32[]{:S(2)}, u32[]{:S(2)}) %all-to-all-start) | async-done | bytes 2097184 | tf_op jit(solution)/shard_map/all_to_all | solution.py:121
  93.9 6.6 %reshape.1023 = bf16[4096,8,32]{2,1,0:T(8,128)(2,1)} reshape(bf16[32,2,16384]{2,1,0:T(2,128)(2,1)S(1)} %all-to-all-done) | data formatting | bytes 4194304
  100.4 9.2 %copy.202 = bf16[32,32,8,128]{3,2,1,0:T(8,128)(2,1)S(1)} copy(bf16[32,32,8,128]{0,2,3,1:T(8,128)(2,1)} %bitcast.224) | data formatting | bytes 4194304 | tf_op jit(solution)/shard_map/all_to_all | solution.py:121
  109.7 3.3 %reshape.979 = bf16[32,256,2,64]{3,2,1,0:T(2,128)(2,1)} reshape(bf16[32,32,8,128]{3,2,1,0:T(8,128)(2,1)S(1)} %copy.202) | data formatting | bytes 4194304 | tf_op jit(solution)/shard_map/reshape | solution.py:129
  113.0 3.7 %fusion.12 = bf16[32,256,2,32]{1,3,2,0:T(8,128)(2,1)S(1)} fusion(bf16[64,32,1,1]{0,1,3,2:T(8,128)(2,1)S(1)} %bitcast.246, bf16[32,256,2,64]{3,2,1,0:T(2,128)(2,1)} %reshape.979), kind=kOutput, calls=%fused_computation.18 | convolution fusion | flops 67633152 | bytes 3149824 | tf_op jit(solution)/shard_map/dot_general | solution.py:128
  116.7 0.6 copy.272
  117.3 1.0 fusion.18
  118.2 0.3 copy.206
  118.5 0.9 copy.207
  119.4 1.2 reshape.1024
  120.6 7.0 %all-to-all-start.1 = ((bf16[32,2,1024]{2,1,0:T(2,128)(2,1)}), bf16[32,2,1024]{2,1,0:T(2,128)(2,1)S(1)}, u32[]{:S(2)}, u32[]{:S(2)}) async-start(bf16[32,2,1024]{2,1,0:T(2,128)(2,1)} %reshape.1024), calls=%async_computation.1 | async-start | bytes 262144 | tf_op jit(solution)/shard_map/all_to_all | solution.py:137
  127.9 0.3 fusion.58
  128.3 8.5 %all-to-all-done.1 = bf16[32,2,1024]{2,1,0:T(2,128)(2,1)S(1)} async-done(((bf16[32,2,1024]{2,1,0:T(2,128)(2,1)}), bf16[32,2,1024]{2,1,0:T(2,128)(2,1)S(1)}, u32[]{:S(2)}, u32[]{:S(2)}) %all-to-all-start.1) | async-done | bytes 131104 | tf_op jit(solution)/shard_map/all_to_all | solution.py:137
  136.8 0.3 reshape.1025
  137.0 0.6 copy.209
  137.6 0.9 reshape.1026
  138.5 7.2 %all-to-all-start.2 = ((bf16[8,2,4096]{2,1,0:T(2,128)(2,1)}), bf16[8,2,4096]{2,1,0:T(2,128)(2,1)S(1)}, u32[]{:S(2)}, u32[]{:S(2)}) async-start(bf16[8,2,4096]{2,1,0:T(2,128)(2,1)} %reshape.1026), calls=%async_computation.2 | async-start | bytes 262144 | tf_op jit(solution)/shard_map/all_to_all | solution.py:136
  145.8 5.7 %all-to-all-done.2 = bf16[8,2,4096]{2,1,0:T(2,128)(2,1)S(1)} async-done(((bf16[8,2,4096]{2,1,0:T(2,128)(2,1)}), bf16[8,2,4096]{2,1,0:T(2,128)(2,1)S(1)}, u32[]{:S(2)}, u32[]{:S(2)}) %all-to-all-start.2) | async-done | bytes 131104 | tf_op jit(solution)/shard_map/all_to_all | solution.py:136
  152.4 0.3 fusion.24
  153.0 0.3 copy.214
  153.3 0.6 reshape.1028
  153.9 12.2 %all_to_all.84 = bf16[32,2,512]{2,1,0:T(2,128)(2,1)S(1)} all-to-all(bf16[32,2,512]{2,1,0:T(2,128)(2,1)S(1)} %reshape.1028), channel_id=1, replica_groups=mesh['dp'=2,'gx'=32,'gy'=8] {'gx'}, dimensions={0} | all-to-all | bytes 131072 | tf_op jit(solution)/shard_map/all_to_all | solution.py:170
  166.0 0.4 reshape.1029
  166.4 0.6 copy.216
  167.0 0.9 reshape.1030
  167.9 5.7 %all-to-all-start.4 = ((bf16[8,2,2048]{2,1,0:T(2,128)(2,1)}), bf16[8,2,2048]{2,1,0:T(2,128)(2,1)S(1)}, u32[]{:S(2)}, u32[]{:S(2)}) async-start(bf16[8,2,2048]{2,1,0:T(2,128)(2,1)} %reshape.1030), calls=%async_computation.4 | async-start | bytes 131072 | tf_op jit(solution)/shard_map/all_to_all | solution.py:169
  173.8 4.9 %all-to-all-done.4 = bf16[8,2,2048]{2,1,0:T(2,128)(2,1)S(1)} async-done(((bf16[8,2,2048]{2,1,0:T(2,128)(2,1)}), bf16[8,2,2048]{2,1,0:T(2,128)(2,1)S(1)}, u32[]{:S(2)}, u32[]{:S(2)}) %all-to-all-start.4) | async-done | bytes 65568 | tf_op jit(solution)/shard_map/all_to_all | solution.py:169
  178.9 0.3 fusion.17
  179.2 0.3 copy.219
  179.5 1.3 copy.220
  180.8 1.5 reshape.1032
  182.4 3.9 %all-to-all-start.5 = ((bf16[32,2,4096]{2,1,0:T(2,128)(2,1)}), bf16[32,2,4096]{2,1,0:T(2,128)(2,1)S(1)}, u32[]{:S(2)}, u32[]{:S(2)}) async-start(bf16[32,2,4096]{2,1,0:T(2,128)(2,1)} %reshape.1032), calls=%async_computation.5 | async-start | bytes 1048576 | tf_op jit(solution)/shard_map/all_to_all | solution.py:183
  186.3 0.3 all-reduce.2.cloned.1.call-start
  186.9 0.6 pad_maximum_fusion.1
  187.6 44.5 %all-reduce.2.cloned.1.call-done = bf16[2,1,32,2,256]{4,2,3,1,0:T(8,128)(2,1)} async-done(((bf16[2,1,32,2,256]{4,2,3,1,0:T(8,128)(2,1)}), bf16[2,1,32,2,256]{4,2,3,1,0:T(8,128)(2,1)}) %all-reduce.2.cloned.1.call-update) | async-done | bytes 65552 | tf_op jit(solution)/shard_map/psum | solution.py:153
  232.1 1.6 copy.230
  233.7 0.7 reshape.1033
  234.4 1.7 copy.222
  236.0 2.7 %reshape.990 = bf16[16,8,64,32]{3,2,1,0:T(8,128)(2,1)S(1)} reshape(bf16[16,8,32,64]{3,2,1,0:T(8,128)(2,1)} %copy.222) | data formatting | bytes 1048576 | tf_op jit(solution)/shard_map/reshape | solution.py:187
  238.7 2.6 %fusion.103 = f32[16,8,64,64]{3,2,1,0:T(8,128)} fusion(bf16[16,8,64,32]{3,2,1,0:T(8,128)(2,1)S(1)} %reshape.990, bf16[32,64,1,1]{1,0,3,2:T(8,128)(2,1)S(1)} %bitcast.247), kind=kOutput, calls=%fused_computation.190 | convolution fusion | flops 33554432 | bytes 2625536 | tf_op jit(solution)/shard_map/dot_general | solution.py:186
  241.4 3.5 %reshape.991 = f32[1,16,8,4096]{3,2,1,0:T(8,128)S(1)} reshape(f32[16,8,64,64]{3,2,1,0:T(8,128)} %fusion.103) | data formatting | bytes 4194304 | tf_op jit(solution)/shard_map/reshape | solution.py:191
  244.9 2.3 fusion.1
  247.2 1.6 copy.229
  (45 shorter events, 2.8 us)
Async XLA Ops:
  7.2 237.8 %copy-start = (bf16[16,16]{1,0:T(8,128)(2,1)S(1)}, bf16[16,16]{1,0:T(8,128)(2,1)}, u32[]{:S(2)}) copy-start(bf16[16,16]{1,0:T(8,128)(2,1)} %param.9) | copy-start | bytes 1540
  7.2 2.3 copy-start.1
  31.1 14.2 %copy-start.2 = (bf16[2,1,32,2,256]{4,3,2,1,0:T(2,128)(2,1)S(1)}, bf16[2,1,32,2,256]{4,3,2,1,0:T(2,128)(2,1)}, u32[]{:S(2)}) copy-start(bf16[2,1,32,2,256]{4,3,2,1,0:T(2,128)(2,1)} %param.8) | copy-start | bytes 196612
  31.1 62.7 %all-to-all-start = ((bf16[32,2,16384]{2,1,0:T(2,128)(2,1)}), bf16[32,2,16384]{2,1,0:T(2,128)(2,1)S(1)}, u32[]{:S(2)}, u32[]{:S(2)}) async-start(bf16[32,2,16384]{2,1,0:T(2,128)(2,1)} %reshape.1022), calls=%async_computation | async-start | bytes 4194304 | tf_op jit(solution)/shard_map/all_to_all | solution.py:121
  120.6 16.2 %all-to-all-start.1 = ((bf16[32,2,1024]{2,1,0:T(2,128)(2,1)}), bf16[32,2,1024]{2,1,0:T(2,128)(2,1)S(1)}, u32[]{:S(2)}, u32[]{:S(2)}) async-start(bf16[32,2,1024]{2,1,0:T(2,128)(2,1)} %reshape.1024), calls=%async_computation.1 | async-start | bytes 262144 | tf_op jit(solution)/shard_map/all_to_all | solution.py:137
  138.5 13.0 %all-to-all-start.2 = ((bf16[8,2,4096]{2,1,0:T(2,128)(2,1)}), bf16[8,2,4096]{2,1,0:T(2,128)(2,1)S(1)}, u32[]{:S(2)}, u32[]{:S(2)}) async-start(bf16[8,2,4096]{2,1,0:T(2,128)(2,1)} %reshape.1026), calls=%async_computation.2 | async-start | bytes 262144 | tf_op jit(solution)/shard_map/all_to_all | solution.py:136
  167.9 10.7 %all-to-all-start.4 = ((bf16[8,2,2048]{2,1,0:T(2,128)(2,1)}), bf16[8,2,2048]{2,1,0:T(2,128)(2,1)S(1)}, u32[]{:S(2)}, u32[]{:S(2)}) async-start(bf16[8,2,2048]{2,1,0:T(2,128)(2,1)} %reshape.1030), calls=%async_computation.4 | async-start | bytes 131072 | tf_op jit(solution)/shard_map/all_to_all | solution.py:169
  182.4 51.3 %all-to-all-start.5 = ((bf16[32,2,4096]{2,1,0:T(2,128)(2,1)}), bf16[32,2,4096]{2,1,0:T(2,128)(2,1)S(1)}, u32[]{:S(2)}, u32[]{:S(2)}) async-start(bf16[32,2,4096]{2,1,0:T(2,128)(2,1)} %reshape.1032), calls=%async_computation.5 | async-start | bytes 1048576 | tf_op jit(solution)/shard_map/all_to_all | solution.py:183
  186.3 45.8 %all-reduce.2.cloned.1.call-start = ((), (), s32[]{:S(2)}) async-start(), calls=%async_computation.6 | async-start | bytes 131072 | tf_op jit(solution)/shard_map/psum | solution.py:153
Sparse Core Ops, SparseCore 0:
  190.5 41.5 all-reduce.1
where the time goes:
time: 257 us; the launch traced here: 256 us
  waiting for transfers between devices  112 us (44%)
  local copies, waits for them, and re-layouts  64.1 us (25%)
  starting transfers between devices  37.9 us (15%)
  between operations  14.5 us (6%)
  blocking collectives  12.2 us (5%)
  matrix products  10.3 us (4%)
  other arithmetic  4.89 us (2%)
    all_to_all x1, waiting for transfers between devices, on_device(): lax.all_to_all(stacked.reshape(stack_rows, local_x, local_yz), 'gx', spli...  48.1 us
    psum x1, waiting for transfers between devices, on_device(): lax.psum(weight_grads(field_hat, grad_scaled).astype(jnp.bfloat16), 'dp')  44.5 us
    unnamed x23, local copies, waits for them, and re-layouts  30.1 us
    all_to_all x1, starting transfers between devices, on_device(): lax.all_to_all(stacked.reshape(stack_rows, local_x, local_yz), 'gx', spli...  13.8 us
    all_to_all x1, blocking collectives, on_device(): lax.all_to_all(back_y, 'gx', split_axis=2, concat_axis=1, tiled=True)  12.2 us
    all_to_all x1, local copies, waits for them, and re-layouts, on_device(): lax.all_to_all(stacked.reshape(stack_rows, local_x, local_yz), 'gx', spli...  9.24 us
    all_to_all x1, waiting for transfers between devices, on_device(): lax.all_to_all(x_spectra, 'gx', split_axis=1, concat_axis=2, tiled=True)  8.52 us
    reshape x1, local copies, waits for them, and re-layouts, on_device(): stacked.reshape(stack_rows, local_x, local_yz)  8.08 us
  transfers between devices with their start and end apart: 6, of which 5 were waited for; matrix products, arithmetic and copies ran while one was open for 2% of the time, Pallas kernels for 0%

commit v1 on v0

v1 whole, which is shorter than its diff:
```python
import math

import jax
import jax.numpy as jnp
import numpy as np
from jax import lax
from jax.experimental import pallas as pl
from jax.experimental.pallas import tpu as pltpu
from jax.sharding import PartitionSpec as P

C = 16
NX = 256
NY = 512
NZ = 64
MX = 32
MY = 32
MZ = 16
GROUP = 8

F32 = jnp.float32
BF16 = jnp.bfloat16
HIGHEST = lax.Precision.HIGHEST


def signed_freqs(kept, length):
    index = np.arange(kept)
    return np.where(index < kept // 2, index, length - kept + index)


def cos_sin(freqs, points, length):
    turns = points[:, None] * freqs[None, :] % length
    angle = turns.astype(np.float32) * np.float32(2.0 * math.pi / length)
    return np.cos(angle).astype(np.float32), np.sin(angle).astype(np.float32)


def z_block_table():
    cosine, sine = cos_sin(np.arange(MZ), np.arange(NZ), NZ)
    parts = np.stack([cosine.T, -sine.T], axis=1)
    same = np.eye(GROUP, dtype=np.float32)
    table = parts[:, :, None, None, :] * same[None, None, :, :, None]
    return table.reshape(2 * MZ * GROUP, GROUP * NZ).astype(BF16)


def y_block_tables(count, local_y, local_mz):
    cosine, sine = cos_sin(signed_freqs(MY, NY), np.arange(NY), NY)
    upper = np.stack([cosine, sine], axis=-1)
    lower = np.stack([-sine, cosine], axis=-1)
    table = np.stack([upper, lower], axis=0)
    table = table.reshape(2, count, local_y, MY, 2).transpose(1, 0, 3, 4, 2)
    same = np.eye(local_mz, dtype=np.float32)
    table = table[:, :, :, None, None, :, :] * same[None, None, None, :, :, None, None]
    return table.reshape(count, 2 * MY * local_mz, local_mz * 2 * local_y).astype(BF16)


def x_row_tables(count, local_x):
    cosine, sine = cos_sin(signed_freqs(MX, NX), np.arange(NX), NX)
    table = np.stack([cosine, sine], axis=0).reshape(2, count, local_x, MX)
    table = table.transpose(1, 0, 3, 2)
    return np.tile(table, (1, 1, 1, 128 // local_x)).astype(BF16)


def dot(left, right, dims, precision=None):
    return lax.dot_general(
        left, right, (dims, ((), ())), preferred_element_type=F32, precision=precision
    )


def gelu_slope(value):
    cdf = 0.5 * (1.0 + lax.erf(value * (1.0 / math.sqrt(2.0))))
    return cdf + value * jnp.exp(-0.5 * value * value) * (1.0 / math.sqrt(2.0 * math.pi))


def forward_zy(where, fields, pre_act, cotangent, z_table, y_table, grad_pre, pieces, lines):
    step = pl.program_id(0)
    slope = gelu_slope(pre_act[...].astype(F32))
    grad = (cotangent[...].astype(F32) * slope).astype(BF16)
    grad_pre[...] = grad
    both = jnp.concatenate([fields[...], grad], axis=0)
    spectra = dot(z_table[...], both, ((1,), (1,)))
    rows = pl.ds(pl.multiple_of(step * GROUP, GROUP), GROUP)
    lines[:, rows, :] = spectra.reshape(2 * MZ, GROUP, both.shape[0])

    @pl.when(step == pl.num_programs(0) - 1)
    def _():
        count = pieces.shape[0]
        per = 2 * MZ // count
        for index in range(count):
            block = lines[index * per : (index + 1) * per]
            block = block.reshape(per * block.shape[1], block.shape[2]).astype(BF16)
            pieces[index] = dot(y_table[0], block, ((1,), (0,))).astype(BF16)


def forward_x(where, arrived, x_rows, pieces):
    count = arrived.shape[0]
    total = arrived[0].astype(F32)
    for index in range(1, count):
        total = total + arrived[index].astype(F32)
    half = total.shape[0] // 2
    swapped = jnp.concatenate([total[half:], -total[:half]], axis=0).astype(BF16)
    total = total.astype(BF16)
    rows = 2 * C
    lanes = total.shape[1]
    local_x = lanes // rows
    owner = lax.broadcasted_iota(jnp.int32, (rows, lanes), 1) // local_x
    mask = owner == lax.broadcasted_iota(jnp.int32, (rows, lanes), 0)
    blocks = []
    for part in range(2):
        table = x_rows[0, part].astype(F32)
        table = jnp.concatenate([table] * (lanes // table.shape[1]), axis=1)
        table = jnp.where(mask[None], table[:, None, :], 0.0)
        blocks.append(table.reshape(MX * rows, lanes).astype(BF16))
    spectra = dot(blocks[0], total, ((1,), (1,))) + dot(blocks[1], swapped, ((1,), (1,)))
    pieces[...] = spectra.reshape(MX, rows, spectra.shape[1]).astype(BF16)


def mode_scale(where, rows, local_mz):
    line = lax.broadcasted_iota(jnp.int32, (rows, 1), 0) % local_mz + where[1] * local_mz
    return jnp.where(line == 0, 1.0, 2.0).astype(F32) / float(NX * NY * NZ)


def repeat_tables():
    lane = lax.broadcasted_iota(jnp.int32, (C, C * C), 1)
    row = lax.broadcasted_iota(jnp.int32, (C, C * C), 0)
    outer = (lane // C == row).astype(F32)
    inner = (lane % C == row).astype(F32)
    return outer, inner


def mode_products(where, arrived, weights, spectrum, grad_hat):
    count = arrived.shape[0]
    total = arrived[0].astype(F32)
    for index in range(1, count):
        total = total + arrived[index].astype(F32)
    total = total.astype(BF16)
    spectrum[...] = total
    modes = total.shape[1] // 2
    outer, inner = repeat_tables()
    grads = dot(total[C:], inner.astype(BF16), ((0,), (0,)))
    scale = mode_scale(where, modes, modes // MY)
    real_d = grads[:modes] * scale
    imag_d = grads[modes:] * scale
    real_w = weights[0].astype(F32)
    imag_w = weights[1].astype(F32)
    products = jnp.concatenate(
        [real_w * real_d + imag_w * imag_d, real_w * imag_d - imag_w * real_d], axis=0
    )
    values = dot(outer, products, ((1,), (1,)), HIGHEST).astype(BF16)
    grad_hat[...] = jnp.broadcast_to(values[None], grad_hat.shape)


def weight_grads(where, own, other, result):
    modes = own.shape[1] // 2
    outer, inner = repeat_tables()
    outer = outer.astype(BF16)
    inner = inner.astype(BF16)
    scale = mode_scale(where, modes, modes // MY)
    real_sum = jnp.zeros((modes, C * C), F32)
    imag_sum = jnp.zeros((modes, C * C), F32)
    for spectrum in (own, other):
        values = spectrum[...]
        field = dot(values[:C], outer, ((0,), (0,)))
        grads = dot(values[C:], inner, ((0,), (0,)))
        real_u, imag_u = field[:modes], field[modes:]
        real_d, imag_d = grads[:modes] * scale, grads[modes:] * scale
        real_sum = real_sum + (real_u * real_d + imag_u * imag_d)
        imag_sum = imag_sum + (real_u * imag_d - imag_u * real_d)
    result[0] = real_sum
    result[1] = imag_sum


def inverse_x(where, arrived, x_rows, result):
    lanes = x_rows.shape[3]
    local_x = lanes // C
    owner = lax.broadcasted_iota(jnp.int32, (C, lanes), 1) // local_x
    mask = owner == lax.broadcasted_iota(jnp.int32, (C, lanes), 0)
    values = arrived[...].reshape(MX * C, arrived.shape[2])
    half = values.shape[1] // 2
    swapped = jnp.concatenate([-values[:, half:], values[:, :half]], axis=1)
    sums = None
    for part, operand in enumerate((values, swapped)):
        table = jnp.where(mask[None], x_rows[0, part].astype(F32)[:, None, :], 0.0)
        table = table.reshape(MX * C, lanes).astype(BF16)
        term = dot(operand, table, ((0,), (0,)))
        sums = term if sums is None else sums + term
    result[...] = jnp.broadcast_to(sums.astype(BF16)[None], result.shape)


def inverse_yz(where, arrived, grad_pre, z_table, y_table, point, result, lines, mixing):
    step = pl.program_id(0)
    rows = mixing.shape[0]
    local_x = rows // C

    @pl.when(step == 0)
    def _():
        count = arrived.shape[0]
        per = 2 * MZ // count
        for index in range(count):
            block = dot(y_table[0], arrived[index], ((0,), (0,)))
            lines[index * per : (index + 1) * per] = block.reshape(per, -1, rows)
        row = lax.broadcasted_iota(jnp.int32, (rows, C), 0) // local_x
        pick = (row == lax.broadcasted_iota(jnp.int32, (rows, C), 1)).astype(BF16)
        spread = dot(pick, point[...], ((1,), (0,))).astype(BF16)
        spread = dot(spread, pick, ((1,), (1,)))
        left = lax.broadcasted_iota(jnp.int32, (rows, rows), 0) % local_x
        right = lax.broadcasted_iota(jnp.int32, (rows, rows), 1) % local_x
        mixing[...] = jnp.where(left == right, spread, 0.0).astype(BF16)

    window = pl.ds(pl.multiple_of(step * GROUP, GROUP), GROUP)
    block = lines[:, window, :].reshape(2 * MZ * GROUP, rows).astype(BF16)
    spectral = dot(block, z_table[...], ((0,), (0,)))
    result[...] = (spectral + dot(mixing[...], grad_pre[...], ((1,), (0,)))).astype(BF16)


def whole(shape):
    return pl.BlockSpec(shape, lambda *_: (0,) * len(shape))


def at_gx(shape):
    return pl.BlockSpec((1,) + shape[1:], lambda i, w: (w[0],) + (0,) * (len(shape) - 1))


def at_gy(shape):
    return pl.BlockSpec((1,) + shape[1:], lambda i, w: (w[1],) + (0,) * (len(shape) - 1))


def call(body, name, grid, in_specs, out_specs, out_shape, scratch=()):
    return pl.pallas_call(
        body,
        name=name,
        grid_spec=pltpu.PrefetchScalarGridSpec(
            num_scalar_prefetch=1,
            grid=(grid,),
            in_specs=in_specs,
            out_specs=out_specs,
            scratch_shapes=scratch,
        ),
        out_shape=out_shape,
        compiler_params=pltpu.CompilerParams(
            dimension_semantics=("arbitrary",), vmem_limit_bytes=16 << 20
        ),
    )


def on_device(fields, pre_act, cotangent, spec_weight, point_weight):
    count_x = lax.axis_size("gx")
    count_y = lax.axis_size("gy")
    _, channels, local_x, local_yz = fields.shape
    local_y = local_yz // NZ
    local_mz = spec_weight.shape[3]
    rows = channels * local_x
    modes = MY * local_mz
    groups = local_y // GROUP
    width = GROUP * NZ
    where = jnp.stack([lax.axis_index("gx"), lax.axis_index("gy")]).astype(jnp.int32)
    z_table = jnp.asarray(z_block_table())
    y_table = jnp.asarray(y_block_tables(count_y, local_y, local_mz))
    x_rows = jnp.asarray(x_row_tables(count_x, local_x))
    shape = jax.ShapeDtypeStruct
    columns = pl.BlockSpec((rows, width), lambda i, w: (0, i))

    grad_pre, pieces = call(
        forward_zy,
        "forward_zy",
        groups,
        [columns, columns, columns, whole(z_table.shape), at_gy(y_table.shape)],
        (columns, whole((count_y, 2 * modes, 2 * rows))),
        (shape((rows, local_yz), BF16), shape((count_y, 2 * modes, 2 * rows), BF16)),
        [pltpu.VMEM((2 * MZ, local_y, 2 * rows), F32)],
    )(
        where,
        fields.reshape(rows, local_yz),
        pre_act.reshape(rows, local_yz),
        cotangent.reshape(rows, local_yz),
        z_table,
        y_table,
    )
    arrived = lax.all_to_all(pieces, "gy", split_axis=0, concat_axis=0, tiled=True)
    pieces = call(
        forward_x,
        "forward_x",
        1,
        [whole(arrived.shape), at_gx(x_rows.shape)],
        whole((MX, 2 * C, 2 * modes)),
        shape((MX, 2 * C, 2 * modes), BF16),
    )(where, arrived, x_rows)
    arrived = lax.all_to_all(pieces, "gx", split_axis=0, concat_axis=0, tiled=True)
    spectrum, grad_hat = call(
        mode_products,
        "mode_products",
        1,
        [whole(arrived.shape), whole((2, modes, C * C))],
        (whole((2 * C, 2 * modes)), whole((count_x, C, 2 * modes))),
        (shape((2 * C, 2 * modes), BF16), shape((count_x, C, 2 * modes), BF16)),
    )(where, arrived, spec_weight.reshape(2, modes, C * C))
    other = lax.ppermute(spectrum, "dp", [(0, 1), (1, 0)])
    gathered = lax.all_to_all(grad_hat, "gx", split_axis=0, concat_axis=0, tiled=True)
    back_x = call(
        inverse_x,
        "inverse_x",
        1,
        [whole(gathered.shape), at_gx(x_rows.shape)],
        whole((count_y, 2 * modes, rows)),
        shape((count_y, 2 * modes, rows), BF16),
    )(where, gathered, x_rows)
    gathered = lax.all_to_all(back_x, "gy", split_axis=0, concat_axis=0, tiled=True)
    grad_spec = call(
        weight_grads,
        "weight_grads",
        1,
        [whole(spectrum.shape), whole(other.shape)],
        whole((2, modes, C * C)),
        shape((2, modes, C * C), F32),
    )(where, spectrum, other)
    grad_fields = call(
        inverse_yz,
        "inverse_yz",
        groups,
        [
            whole(gathered.shape),
            columns,
            whole(z_table.shape),
            at_gy(y_table.shape),
            whole(point_weight.shape),
        ],
        columns,
        shape((rows, local_yz), BF16),
        [pltpu.VMEM((2 * MZ, local_y, rows), F32), pltpu.VMEM((rows, rows), BF16)],
    )(where, gathered, grad_pre, z_table, y_table, point_weight)
    return grad_fields.reshape(fields.shape), grad_spec.reshape(spec_weight.shape)


def solution(mesh):
    placed = (
        P("dp", None, "gx", "gy"),
        P("dp", None, "gx", "gy"),
        P("dp", None, "gx", "gy"),
        P(None, "gx", None, "gy", None),
        P(),
    )
    return jax.shard_map(
        on_device,
        mesh=mesh,
        in_specs=placed,
        out_specs=(P("dp", None, "gx", "gy"), P(None, "gx", None, "gy", None)),
        check_vma=False,
    )
```

time: 257 us -> 95.6 us (0.37)
  waiting for transfers between devices: 112 us -> 13 us
  local copies, waits for them, and re-layouts: 64.1 us -> 6.45 us
  blocking collectives: 12.2 us -> 38.7 us
  starting transfers between devices: 37.9 us -> 21.9 us
  Pallas kernels: 0 us -> 14 us
  between operations: 14.5 us -> 0.72 us
  matrix products: 10.3 us -> 0 us
  other arithmetic: 4.89 us -> 0.08 us
    all_to_all x5 -> x2, waiting for transfers between devices: 67.2 us -> 9.61 us  [the longest x1 9.61 us: on_device(): lax.all_to_all(pieces, 'gx', split_axis=0, concat_axis=0, tiled=True)]
    psum x1 -> x0, waiting for transfers between devices: 44.5 us -> none  [on_device(): lax.psum(weight_grads(field_hat, grad_scaled).astype(jnp.bfloat16), 'dp')]
    all_to_all x1 -> x2, blocking collectives: 12.2 us -> 38.7 us  [the longest x1 23.7 us: on_device(): lax.all_to_all(pieces, 'gy', split_axis=0, concat_axis=0, tiled=True)]
    unnamed x23 -> x20, local copies, waits for them, and re-layouts: 30.1 us -> 5.69 us
    all_to_all x5 -> x2, starting transfers between devices: 37.6 us -> 16.6 us  [the longest x1 9.94 us: on_device(): lax.all_to_all(pieces, 'gx', split_axis=0, concat_axis=0, tiled=True)]
    reshape x8 -> x2, local copies, waits for them, and re-layouts: 20.7 us -> 0.76 us  [the longest x1 0.73 us: on_device(): grad_spec.reshape(spec_weight.shape)]
    pallas_call x0 -> x6, Pallas kernels: none -> 14 us  [the longest x1 4.88 us: on_device(): call(inverse_yz, 'inverse_yz', groups, [whole(gathered.shape), columns, w...]
    all_to_all x6 -> x0, local copies, waits for them, and re-layouts: 12.3 us -> none  [the longest x1 9.24 us: on_device(): lax.all_to_all(stacked.reshape(stack_rows, local_x, local_yz), 'gx', spli...]
  transfers between devices with their start and end apart: 6 -> 3, of which waited for: 5 -> 2; matrix products, arithmetic and copies ran while one was open for 2% -> 1% of each run, Pallas kernels for 0% -> 1%
where the time goes in v1:
time: 95.6 us; the launch traced here: 94.9 us
  blocking collectives  38.7 us (40%)
  starting transfers between devices  21.9 us (23%)
  Pallas kernels  14 us (15%)
  waiting for transfers between devices  13 us (14%)
  local copies, waits for them, and re-layouts  6.45 us (7%)
    all_to_all x1, blocking collectives, on_device(): lax.all_to_all(pieces, 'gy', split_axis=0, concat_axis=0, tiled=True)  23.7 us
    all_to_all x1, blocking collectives, on_device(): lax.all_to_all(grad_hat, 'gx', split_axis=0, concat_axis=0, tiled=True)  15.1 us
    all_to_all x1, starting transfers between devices, on_device(): lax.all_to_all(pieces, 'gx', split_axis=0, concat_axis=0, tiled=True)  9.94 us
    all_to_all x1, waiting for transfers between devices, on_device(): lax.all_to_all(pieces, 'gx', split_axis=0, concat_axis=0, tiled=True)  9.61 us
    all_to_all x1, starting transfers between devices, on_device(): lax.all_to_all(back_x, 'gy', split_axis=0, concat_axis=0, tiled=True)  6.69 us
    unnamed x20, local copies, waits for them, and re-layouts  5.69 us
    ppermute x1, starting transfers between devices, on_device(): other = lax.ppermute(spectrum, 'dp', [(0, 1), (1, 0)])  5.31 us
    pallas_call x1, Pallas kernels, on_device(): call(inverse_yz, 'inverse_yz', groups, [whole(gathered.shape), columns, w...  4.88 us
  transfers between devices with their start and end apart: 3, of which 2 were waited for; matrix products, arithmetic and copies ran while one was open for 1% of the time, Pallas kernels for 1%

profile of v1, /device:TPU:1, one launch (start us, length us, event | category | flops | bytes accessed | tf_op | source)
XLA Modules:
  0.0 94.9 jit_solution(830509920764667766)
XLA Ops:
  0.6 0.1 pad_add_fusion.where
  0.7 0.0 copy-start.1
  0.7 1.0 %copy-done.1 = bf16[8,128,256]{2,1,0:T(8,128)(2,1)S(1)} copy-done((bf16[8,128,256]{2,1,0:T(8,128)(2,1)S(1)}, bf16[8,128,256]{2,1,0:T(8,128)(2,1)}, u32[]{:S(2)}) %copy-start.1) | copy-done | bytes 524312
  1.8 0.0 copy-start.3
  1.8 1.2 %copy-done.3 = bf16[1,16,8,4096]{3,2,1,0:T(8,128)(2,1)S(1)} copy-done((bf16[1,16,8,4096]{3,2,1,0:T(8,128)(2,1)S(1)}, bf16[1,16,8,4096]{3,2,1,0:T(8,128)(2,1)}, u32[]{:S(2)}) %copy-start.3) | copy-done | bytes 1048600
  3.0 0.0 copy-start.4
  3.0 1.2 %copy-done.4 = bf16[1,16,8,4096]{3,2,1,0:T(8,128)(2,1)S(1)} copy-done((bf16[1,16,8,4096]{3,2,1,0:T(8,128)(2,1)S(1)}, bf16[1,16,8,4096]{3,2,1,0:T(8,128)(2,1)}, u32[]{:S(2)}) %copy-start.4) | copy-done | bytes 1048600
  4.2 0.0 copy-start.5
  4.2 1.2 %copy-done.5 = bf16[1,16,8,4096]{3,2,1,0:T(8,128)(2,1)S(1)} copy-done((bf16[1,16,8,4096]{3,2,1,0:T(8,128)(2,1)S(1)}, bf16[1,16,8,4096]{3,2,1,0:T(8,128)(2,1)}, u32[]{:S(2)}) %copy-start.5) | copy-done | bytes 1048600
  5.4 0.0 copy-start.6
  5.4 0.9 copy-done.6
  6.4 4.0 %forward_zy.1 = (bf16[128,4096]{1,0:T(8,128)(2,1)S(1)}, bf16[8,128,256]{2,1,0:T(8,128)(2,1)S(1)}) custom-call(s32[2]{0:T(128)S(1)} %pad_add_fusion.where, bf16[128,4096]{1,0:T(8,128)(2,1)S(1)} %bitcast.7, bf16[128,4096]{1,0:T(8,128)(2,1)S(1)} %bitcast.8, bf16[128,4096]{1,0:T(8,128)(2,1)S(1)} %bitcast.9, bf16[256,512]{1,0:T(8,128)(2,1)S(1)} %copy-done.6, ...), custom_call_target="tpu_custom_call" | custom-call | tf_op jit(solution)/shard_map/forward_zy/pallas_call | solution.py:261
  10.4 0.0 copy-start
  10.4 23.7 %all_to_all.20.arrived = bf16[8,128,256]{2,1,0:T(8,128)(2,1)S(1)} all-to-all(bf16[8,128,256]{2,1,0:T(8,128)(2,1)S(1)} %get-tuple-element.6), channel_id=1, replica_groups=mesh['dp'=2,'gx'=32,'gy'=8] {'gy'}, dimensions={0} | all-to-all | bytes 1048576 | tf_op jit(solution)/shard_map/all_to_all | solution.py:277
  34.0 0.0 copy-done
  34.0 1.7 %forward_x.1 = bf16[32,32,128]{2,1,0:T(8,128)(2,1)} custom-call(s32[2]{0:T(128)S(1)} %pad_add_fusion.where, bf16[8,128,256]{2,1,0:T(8,128)(2,1)S(1)} %all_to_all.20.arrived, bf16[32,2,32,128]{3,2,1,0:T(8,128)(2,1)S(1)} %copy-done), custom_call_target="tpu_custom_call" | custom-call | tf_op jit(solution)/shard_map/forward_x/pallas_call | solution.py:278
  35.8 0.0 copy-start.9
  35.8 9.9 %all-to-all-start.1 = ((bf16[32,32,128]{2,1,0:T(8,128)(2,1)}), bf16[32,32,128]{2,1,0:T(8,128)(2,1)S(1)}, u32[]{:S(2)}, u32[]{:S(2)}) async-start(bf16[32,32,128]{2,1,0:T(8,128)(2,1)} %forward_x.1), calls=%async_computation.1 | async-start | bytes 524288 | tf_op jit(solution)/shard_map/all_to_all | solution.py:286
  45.7 0.0 copy-done.9
  45.8 9.6 %all-to-all-done.1.arrived = bf16[32,32,128]{2,1,0:T(8,128)(2,1)S(1)} async-done(((bf16[32,32,128]{2,1,0:T(8,128)(2,1)}), bf16[32,32,128]{2,1,0:T(8,128)(2,1)S(1)}, u32[]{:S(2)}, u32[]{:S(2)}) %all-to-all-start.1) | async-done | bytes 262176 | tf_op jit(solution)/shard_map/all_to_all | solution.py:286
  55.4 1.0 %mode_products.1 = (bf16[32,128]{1,0:T(8,128)(2,1)S(1)}, bf16[32,16,128]{2,1,0:T(8,128)(2,1)S(1)}) custom-call(s32[2]{0:T(128)S(1)} %pad_add_fusion.where, bf16[32,32,128]{2,1,0:T(8,128)(2,1)S(1)} %all-to-all-done.1.arrived, bf16[2,64,256]{2,1,0:T(8,128)(2,1)S(1)} %reshape.25.weights), custom_call_target="tpu_custom_call" | custom-call | tf_op jit(solution)/shard_map/mode_products/pallas_call | solution.py:287
  56.4 15.1 %all_to_all.21.arrived = bf16[32,16,128]{2,1,0:T(8,128)(2,1)S(1)} all-to-all(bf16[32,16,128]{2,1,0:T(8,128)(2,1)S(1)} %get-tuple-element.7), channel_id=1, replica_groups=mesh['dp'=2,'gx'=32,'gy'=8] {'gx'}, dimensions={0} | all-to-all | bytes 262144 | tf_op jit(solution)/shard_map/all_to_all | solution.py:296
  71.5 1.6 %inverse_x.1 = bf16[8,128,128]{2,1,0:T(8,128)(2,1)} custom-call(s32[2]{0:T(128)S(1)} %pad_add_fusion.where, bf16[32,16,128]{2,1,0:T(8,128)(2,1)S(1)} %all_to_all.21.arrived, bf16[32,2,32,128]{3,2,1,0:T(8,128)(2,1)S(1)} %copy-done), custom_call_target="tpu_custom_call" | custom-call | tf_op jit(solution)/shard_map/inverse_x/pallas_call | solution.py:297
  73.1 0.0 copy-start.2
  73.1 6.7 %all-to-all-start.3 = ((bf16[8,128,128]{2,1,0:T(8,128)(2,1)}), bf16[8,128,128]{2,1,0:T(8,128)(2,1)S(1)}, u32[]{:S(2)}, u32[]{:S(2)}) async-start(bf16[8,128,128]{2,1,0:T(8,128)(2,1)} %inverse_x.1), calls=%async_computation.3 | async-start | bytes 524288 | tf_op jit(solution)/shard_map/all_to_all | solution.py:305
  79.8 0.0 copy-start.7
  79.8 5.3 %collective-permute-start = (bf16[32,128]{1,0:T(8,128)(2,1)S(1)}, bf16[32,128]{1,0:T(8,128)(2,1)S(1)}, u32[]{:S(2)}, u32[]{:S(2)}) collective-permute-start(bf16[32,128]{1,0:T(8,128)(2,1)S(1)} %get-tuple-element.9.own), channel_id=1, source_target_pairs={{0,256},{256,0},{1,257},{257,1},{2,258},{258,2},{3,259},{259,3},{4... | collective-permute-start | bytes 24584 | tf_op jit(solution)/shard_map/ppermute | solution.py:295
  85.1 3.4 %collective-permute-done.other = bf16[32,128]{1,0:T(8,128)(2,1)S(1)} collective-permute-done((bf16[32,128]{1,0:T(8,128)(2,1)S(1)}, bf16[32,128]{1,0:T(8,128)(2,1)S(1)}, u32[]{:S(2)}, u32[]{:S(2)}) %collective-permute-start) | collective-permute-done | bytes 8224 | tf_op jit(solution)/shard_map/ppermute | solution.py:295
  88.5 0.8 weight_grads.1
  89.3 0.0 copy-start.8
  89.3 0.7 reshape.27
  90.0 0.0 all-to-all-done.3.arrived
  90.0 0.0 copy-done.2
  90.0 0.0 copy-done.7
  90.0 0.0 copy-done.8
  90.0 4.9 %inverse_yz.1 = bf16[128,4096]{1,0:T(8,128)(2,1)} custom-call(s32[2]{0:T(128)S(1)} %pad_add_fusion.where, bf16[8,128,128]{2,1,0:T(8,128)(2,1)S(1)} %all-to-all-done.3.arrived, bf16[128,4096]{1,0:T(8,128)(2,1)S(1)} %get-tuple-element.8.grad_pre, bf16[256,512]{1,0:T(8,128)(2,1)S(1)} %copy-done.7, bf16[8,128,256]{2,1,0:T(8,128)(2,1)S(1)} %copy-done.2, ...), custom_call_target="tpu_custom_call" | custom-call | tf_op jit(solution)/shard_map/inverse_yz/pallas_call | solution.py:314
  (1 shorter events, 0.0 us)
Async XLA Ops:
  0.7 1.0 %copy-start.1 = (bf16[8,128,256]{2,1,0:T(8,128)(2,1)S(1)}, bf16[8,128,256]{2,1,0:T(8,128)(2,1)}, u32[]{:S(2)}) copy-start(bf16[8,128,256]{2,1,0:T(8,128)(2,1)} %constant.16.clone.y_table) | copy-start | bytes 1572868
  1.8 1.2 %copy-start.3 = (bf16[1,16,8,4096]{3,2,1,0:T(8,128)(2,1)S(1)}, bf16[1,16,8,4096]{3,2,1,0:T(8,128)(2,1)}, u32[]{:S(2)}) copy-start(bf16[1,16,8,4096]{3,2,1,0:T(8,128)(2,1)} %param.8) | copy-start | bytes 3145732
  3.0 1.2 %copy-start.4 = (bf16[1,16,8,4096]{3,2,1,0:T(8,128)(2,1)S(1)}, bf16[1,16,8,4096]{3,2,1,0:T(8,128)(2,1)}, u32[]{:S(2)}) copy-start(bf16[1,16,8,4096]{3,2,1,0:T(8,128)(2,1)} %param.9) | copy-start | bytes 3145732
  4.2 1.2 %copy-start.5 = (bf16[1,16,8,4096]{3,2,1,0:T(8,128)(2,1)S(1)}, bf16[1,16,8,4096]{3,2,1,0:T(8,128)(2,1)}, u32[]{:S(2)}) copy-start(bf16[1,16,8,4096]{3,2,1,0:T(8,128)(2,1)} %param.10) | copy-start | bytes 3145732
  5.4 0.9 %copy-start.6 = (bf16[256,512]{1,0:T(8,128)(2,1)S(1)}, bf16[256,512]{1,0:T(8,128)(2,1)}, u32[]{:S(2)}) copy-start(bf16[256,512]{1,0:T(8,128)(2,1)} %constant.15.clone.z_table) | copy-start | bytes 786436
  10.4 23.7 %copy-start = (bf16[32,2,32,128]{3,2,1,0:T(8,128)(2,1)S(1)}, bf16[32,2,32,128]{3,2,1,0:T(8,128)(2,1)}, u32[]{:S(2)}) copy-start(bf16[32,2,32,128]{3,2,1,0:T(8,128)(2,1)} %constant.17.clone.x_rows) | copy-start | bytes 1572868
  35.8 9.9 %copy-start.9 = (bf16[2,1,32,2,256]{4,3,2,1,0:T(2,128)(2,1)S(1)}, bf16[2,1,32,2,256]{4,3,2,1,0:T(2,128)(2,1)}, u32[]{:S(2)}) copy-start(bf16[2,1,32,2,256]{4,3,2,1,0:T(2,128)(2,1)} %param.11) | copy-start | bytes 196612
  35.8 19.6 %all-to-all-start.1 = ((bf16[32,32,128]{2,1,0:T(8,128)(2,1)}), bf16[32,32,128]{2,1,0:T(8,128)(2,1)S(1)}, u32[]{:S(2)}, u32[]{:S(2)}) async-start(bf16[32,32,128]{2,1,0:T(8,128)(2,1)} %forward_x.1), calls=%async_computation.1 | async-start | bytes 524288 | tf_op jit(solution)/shard_map/all_to_all | solution.py:286
  73.1 16.9 %copy-start.2 = (bf16[8,128,256]{2,1,0:T(8,128)(2,1)S(1)}, bf16[8,128,256]{2,1,0:T(8,128)(2,1)}, u32[]{:S(2)}) copy-start(bf16[8,128,256]{2,1,0:T(8,128)(2,1)} %constant.16.clone.y_table) | copy-start | bytes 1572868
  73.1 16.9 %all-to-all-start.3 = ((bf16[8,128,128]{2,1,0:T(8,128)(2,1)}), bf16[8,128,128]{2,1,0:T(8,128)(2,1)S(1)}, u32[]{:S(2)}, u32[]{:S(2)}) async-start(bf16[8,128,128]{2,1,0:T(8,128)(2,1)} %inverse_x.1), calls=%async_computation.3 | async-start | bytes 524288 | tf_op jit(solution)/shard_map/all_to_all | solution.py:305
  79.8 10.2 %copy-start.7 = (bf16[256,512]{1,0:T(8,128)(2,1)S(1)}, bf16[256,512]{1,0:T(8,128)(2,1)}, u32[]{:S(2)}) copy-start(bf16[256,512]{1,0:T(8,128)(2,1)} %constant.15.clone.z_table) | copy-start | bytes 786436
  79.8 8.7 %collective-permute-start = (bf16[32,128]{1,0:T(8,128)(2,1)S(1)}, bf16[32,128]{1,0:T(8,128)(2,1)S(1)}, u32[]{:S(2)}, u32[]{:S(2)}) collective-permute-start(bf16[32,128]{1,0:T(8,128)(2,1)S(1)} %get-tuple-element.9.own), channel_id=1, source_target_pairs={{0,256},{256,0},{1,257},{257,1},{2,258},{258,2},{3,259},{259,3},{4... | collective-permute-start | bytes 24584 | tf_op jit(solution)/shard_map/ppermute | solution.py:295
  89.3 0.8 copy-start.8

commit v2 on v1

--- a/solution.py
+++ b/solution.py
@@ -70,44 +70,81 @@
     return cdf + value * jnp.exp(-0.5 * value * value) * (1.0 / math.sqrt(2.0 * math.pi))
 
 
-def forward_zy(where, fields, pre_act, cotangent, z_table, y_table, grad_pre, pieces, lines):
+def transform_group(block, z_table, y_table, store, count, lines):
     step = pl.program_id(0)
+    for index in range(block.shape[1] // z_table.shape[1]):
+        width = z_table.shape[1]
+        part = block[:, index * width : (index + 1) * width]
+        spectra = dot(z_table[...], part, ((1,), (1,)))
+        start = pl.multiple_of(step * (block.shape[1] // NZ), GROUP) + index * GROUP
+        lines[:, pl.ds(start, GROUP), :] = spectra.reshape(2 * MZ, GROUP, block.shape[0])
+
+    @pl.when(step == pl.num_programs(0) - 1)
+    def _():
+        per = 2 * MZ // count
+        for index in range(count):
+            chunk = lines[index * per : (index + 1) * per]
+            chunk = chunk.reshape(per * chunk.shape[1], chunk.shape[2]).astype(BF16)
+            store(index, dot(y_table[0], chunk, ((1,), (0,))).astype(BF16))
+
+
+def forward_grads(where, pre_act, cotangent, z_table, y_table, grad_pre, pieces, lines):
     slope = gelu_slope(pre_act[...].astype(F32))
     grad = (cotangent[...].astype(F32) * slope).astype(BF16)
     grad_pre[...] = grad
-    both = jnp.concatenate([fields[...], grad], axis=0)
-    spectra = dot(z_table[...], both, ((1,), (1,)))
-    rows = pl.ds(pl.multiple_of(step * GROUP, GROUP), GROUP)
-    lines[:, rows, :] = spectra.reshape(2 * MZ, GROUP, both.shape[0])
-
-    @pl.when(step == pl.num_programs(0) - 1)
-    def _():
-        count = pieces.shape[0]
-        per = 2 * MZ // count
-        for index in range(count):
-            block = lines[index * per : (index + 1) * per]
-            block = block.reshape(per * block.shape[1], block.shape[2]).astype(BF16)
-            pieces[index] = dot(y_table[0], block, ((1,), (0,))).astype(BF16)
+
+    def store(index, value):
+        pieces[index] = value
+
+    transform_group(grad, z_table, y_table, store, pieces.shape[0], lines)
+
+
+def forward_fields(where, fields, z_table, y_table, kept, given, lines):
+    side = where[1] % 2
+
+    def store(index, value):
+        @pl.when(side == index % 2)
+        def _():
+            kept[index // 2] = value
+
+        @pl.when(side != index % 2)
+        def _():
+            given[index // 2] = value
+
+    transform_group(fields[...], z_table, y_table, store, 2 * kept.shape[0], lines)
+
+
+def add_halves(where, kept, taken, *sums):
+    chip = where[1] // 2
+    for distance, total in enumerate(sums):
+        index = lax.rem(chip + distance, len(sums))
+        total[...] = (kept[index].astype(F32) + taken[index].astype(F32)).astype(BF16)
+
+
+def forward_fields_x(where, *refs):
+    lines, x_rows, pieces = refs[:-2], refs[-2], refs[-1]
+    total = lines[0][...].astype(F32)
+    for term in lines[1:]:
+        total = total + term[...].astype(F32)
+    transform_x(total, x_rows, pieces)
 
 
 def forward_x(where, arrived, x_rows, pieces):
-    count = arrived.shape[0]
-    total = arrived[0].astype(F32)
-    for index in range(1, count):
-        total = total + arrived[index].astype(F32)
+    transform_x(add_up(arrived), x_rows, pieces)
+
+
+def transform_x(total, x_rows, pieces):
     half = total.shape[0] // 2
     swapped = jnp.concatenate([total[half:], -total[:half]], axis=0).astype(BF16)
     total = total.astype(BF16)
-    rows = 2 * C
+    rows = C
     lanes = total.shape[1]
     local_x = lanes // rows
     owner = lax.broadcasted_iota(jnp.int32, (rows, lanes), 1) // local_x
     mask = owner == lax.broadcasted_iota(jnp.int32, (rows, lanes), 0)
     blocks = []
     for part in range(2):
-        table = x_rows[0, part].astype(F32)
-        table = jnp.concatenate([table] * (lanes // table.shape[1]), axis=1)
-        table = jnp.where(mask[None], table[:, None, :], 0.0)
+        table = jnp.where(mask[None], x_rows[0, part].astype(F32)[:, None, :], 0.0)
         blocks.append(table.reshape(MX * rows, lanes).astype(BF16))
     spectra = dot(blocks[0], total, ((1,), (1,))) + dot(blocks[1], swapped, ((1,), (1,)))
     pieces[...] = spectra.reshape(MX, rows, spectra.shape[1]).astype(BF16)
@@ -126,16 +163,19 @@
     return outer, inner
 
 
-def mode_products(where, arrived, weights, spectrum, grad_hat):
-    count = arrived.shape[0]
-    total = arrived[0].astype(F32)
-    for index in range(1, count):
-        total = total + arrived[index].astype(F32)
-    total = total.astype(BF16)
+def add_up(arrived, rows=slice(None)):
+    total = arrived[0, rows].astype(F32)
+    for index in range(1, arrived.shape[0]):
+        total = total + arrived[index, rows].astype(F32)
+    return total
+
+
+def mode_products(where, arrived, weights, fields, spectrum, pieces):
+    total = add_up(arrived).astype(BF16)
     spectrum[...] = total
     modes = total.shape[1] // 2
     outer, inner = repeat_tables()
-    grads = dot(total[C:], inner.astype(BF16), ((0,), (0,)))
+    grads = dot(total, inner.astype(BF16), ((0,), (0,)))
     scale = mode_scale(where, modes, modes // MY)
     real_d = grads[:modes] * scale
     imag_d = grads[modes:] * scale
@@ -145,7 +185,13 @@
         [real_w * real_d + imag_w * imag_d, real_w * imag_d - imag_w * real_d], axis=0
     )
     values = dot(outer, products, ((1,), (1,)), HIGHEST).astype(BF16)
-    grad_hat[...] = jnp.broadcast_to(values[None], grad_hat.shape)
+    pieces[:, :C] = jnp.broadcast_to(values[None], fields.shape)
+    pieces[:, C:] = fields[...]
+
+
+def join_spectra(where, arrived, grads, spectra):
+    spectra[:C] = add_up(arrived, slice(C, None)).astype(BF16)
+    spectra[C:] = grads[...]
 
 
 def weight_grads(where, own, other, result):
@@ -156,8 +202,8 @@
     scale = mode_scale(where, modes, modes // MY)
     real_sum = jnp.zeros((modes, C * C), F32)
     imag_sum = jnp.zeros((modes, C * C), F32)
-    for spectrum in (own, other):
-        values = spectrum[...]
+    for spectra in (own, other):
+        values = spectra[...]
         field = dot(values[:C], outer, ((0,), (0,)))
         grads = dot(values[C:], inner, ((0,), (0,)))
         real_u, imag_u = field[:modes], field[modes:]
@@ -173,7 +219,7 @@
     local_x = lanes // C
     owner = lax.broadcasted_iota(jnp.int32, (C, lanes), 1) // local_x
     mask = owner == lax.broadcasted_iota(jnp.int32, (C, lanes), 0)
-    values = arrived[...].reshape(MX * C, arrived.shape[2])
+    values = arrived[:, :C].reshape(MX * C, arrived.shape[2])
     half = values.shape[1] // 2
     swapped = jnp.concatenate([-values[:, half:], values[:, :half]], axis=1)
     sums = None
@@ -205,10 +251,14 @@
         right = lax.broadcasted_iota(jnp.int32, (rows, rows), 1) % local_x
         mixing[...] = jnp.where(left == right, spread, 0.0).astype(BF16)
 
-    window = pl.ds(pl.multiple_of(step * GROUP, GROUP), GROUP)
-    block = lines[:, window, :].reshape(2 * MZ * GROUP, rows).astype(BF16)
-    spectral = dot(block, z_table[...], ((0,), (0,)))
-    result[...] = (spectral + dot(mixing[...], grad_pre[...], ((1,), (0,)))).astype(BF16)
+    width = z_table.shape[1]
+    for index in range(result.shape[1] // width):
+        start = pl.multiple_of(step * (result.shape[1] // NZ), GROUP) + index * GROUP
+        block = lines[:, pl.ds(start, GROUP), :].reshape(2 * MZ * GROUP, rows).astype(BF16)
+        spectral = dot(block, z_table[...], ((0,), (0,)))
+        part = slice(index * width, (index + 1) * width)
+        mixed = dot(mixing[...], grad_pre[:, part], ((1,), (0,)))
+        result[:, part] = (spectral + mixed).astype(BF16)
 
 
 def whole(shape):
@@ -223,10 +273,9 @@
     return pl.BlockSpec((1,) + shape[1:], lambda i, w: (w[1],) + (0,) * (len(shape) - 1))
 
 
-def call(body, name, grid, in_specs, out_specs, out_shape, scratch=()):
+def call(body, grid, in_specs, out_specs, out_shape, scratch=(), vmem=16):
     return pl.pallas_call(
         body,
-        name=name,
         grid_spec=pltpu.PrefetchScalarGridSpec(
             num_scalar_prefetch=1,
             grid=(grid,),
@@ -236,9 +285,13 @@
         ),
         out_shape=out_shape,
         compiler_params=pltpu.CompilerParams(
-            dimension_semantics=("arbitrary",), vmem_limit_bytes=16 << 20
+            dimension_semantics=("arbitrary",), vmem_limit_bytes=vmem << 20
         ),
     )
+
+
+def exchange(pieces, axis):
+    return lax.all_to_all(pieces, axis, split_axis=0, concat_axis=0, tiled=True)
 
 
 def on_device(fields, pre_act, cotangent, spec_weight, point_weight):
@@ -249,82 +302,105 @@
     local_mz = spec_weight.shape[3]
     rows = channels * local_x
     modes = MY * local_mz
-    groups = local_y // GROUP
-    width = GROUP * NZ
+    steps = 4
     where = jnp.stack([lax.axis_index("gx"), lax.axis_index("gy")]).astype(jnp.int32)
     z_table = jnp.asarray(z_block_table())
     y_table = jnp.asarray(y_block_tables(count_y, local_y, local_mz))
     x_rows = jnp.asarray(x_row_tables(count_x, local_x))
     shape = jax.ShapeDtypeStruct
-    columns = pl.BlockSpec((rows, width), lambda i, w: (0, i))
-
-    grad_pre, pieces = call(
-        forward_zy,
-        "forward_zy",
-        groups,
-        [columns, columns, columns, whole(z_table.shape), at_gy(y_table.shape)],
-        (columns, whole((count_y, 2 * modes, 2 * rows))),
-        (shape((rows, local_yz), BF16), shape((count_y, 2 * modes, 2 * rows), BF16)),
-        [pltpu.VMEM((2 * MZ, local_y, 2 * rows), F32)],
+    columns = pl.BlockSpec((rows, local_yz // steps), lambda i, w: (0, i))
+    y_pieces = (count_y, 2 * modes, rows)
+    x_pieces = (count_x, C, 2 * modes)
+    lines = pltpu.VMEM((2 * MZ, local_y, rows), F32)
+    tables = [whole(z_table.shape), at_gy(y_table.shape)]
+
+    grad_pre, grad_lines = call(
+        forward_grads,
+        steps,
+        [columns, columns] + tables,
+        (columns, whole(y_pieces)),
+        (shape((rows, local_yz), BF16), shape(y_pieces, BF16)),
+        [lines],
+        vmem=60,
     )(
         where,
-        fields.reshape(rows, local_yz),
         pre_act.reshape(rows, local_yz),
         cotangent.reshape(rows, local_yz),
         z_table,
         y_table,
     )
-    arrived = lax.all_to_all(pieces, "gy", split_axis=0, concat_axis=0, tiled=True)
-    pieces = call(
-        forward_x,
-        "forward_x",
+    grad_lines = exchange(grad_lines, "gy")
+    half = (count_y // 2,) + y_pieces[1:]
+    line = y_pieces[1:]
+    kept, given = call(
+        forward_fields,
+        steps,
+        [columns] + tables,
+        (whole(half), whole(half)),
+        (shape(half, BF16), shape(half, BF16)),
+        [lines],
+        vmem=60,
+    )(where, fields.reshape(rows, local_yz), z_table, y_table)
+    taken = lax.ppermute(given, "gy", [(i, i ^ 1) for i in range(count_y)])
+    field_lines = call(
+        add_halves,
         1,
-        [whole(arrived.shape), at_gx(x_rows.shape)],
-        whole((MX, 2 * C, 2 * modes)),
-        shape((MX, 2 * C, 2 * modes), BF16),
+        [whole(half), whole(half)],
+        (whole(line),) * half[0],
+        (shape(line, BF16),) * half[0],
+    )(where, kept, taken)
+    field_lines = [field_lines[0]] + [
+        lax.ppermute(
+            field_lines[k], "gy", [(i, (i + 2 * k) % count_y) for i in range(count_y)]
+        )
+        for k in range(1, half[0])
+    ]
+    field_modes = call(
+        forward_fields_x,
+        1,
+        [whole(line)] * half[0] + [at_gx(x_rows.shape)],
+        whole(x_pieces),
+        shape(x_pieces, BF16),
+    )(where, *field_lines, x_rows)
+    grad_modes = call(
+        forward_x, 1, [whole(y_pieces), at_gx(x_rows.shape)], whole(x_pieces), shape(x_pieces, BF16)
+    )(where, grad_lines, x_rows)
+    grad_modes = exchange(grad_modes, "gx")
+    both = (count_x, 2 * C, 2 * modes)
+    grad_spectrum, pieces = call(
+        mode_products,
+        1,
+        [whole(x_pieces), whole((2, modes, C * C)), whole(x_pieces)],
+        (whole((C, 2 * modes)), whole(both)),
+        (shape((C, 2 * modes), BF16), shape(both, BF16)),
+    )(where, grad_modes, spec_weight.reshape(2, modes, C * C), field_modes)
+    arrived = exchange(pieces, "gx")
+    back_x = call(
+        inverse_x, 1, [whole(both), at_gx(x_rows.shape)], whole(y_pieces), shape(y_pieces, BF16)
     )(where, arrived, x_rows)
-    arrived = lax.all_to_all(pieces, "gx", split_axis=0, concat_axis=0, tiled=True)
-    spectrum, grad_hat = call(
-        mode_products,
-        "mode_products",
+    gathered = exchange(back_x, "gy")
+    spectra = call(
+        join_spectra,
         1,
-        [whole(arrived.shape), whole((2, modes, C * C))],
-        (whole((2 * C, 2 * modes)), whole((count_x, C, 2 * modes))),
-        (shape((2 * C, 2 * modes), BF16), shape((count_x, C, 2 * modes), BF16)),
-    )(where, arrived, spec_weight.reshape(2, modes, C * C))
-    other = lax.ppermute(spectrum, "dp", [(0, 1), (1, 0)])
-    gathered = lax.all_to_all(grad_hat, "gx", split_axis=0, concat_axis=0, tiled=True)
-    back_x = call(
-        inverse_x,
-        "inverse_x",
-        1,
-        [whole(gathered.shape), at_gx(x_rows.shape)],
-        whole((count_y, 2 * modes, rows)),
-        shape((count_y, 2 * modes, rows), BF16),
-    )(where, gathered, x_rows)
-    gathered = lax.all_to_all(back_x, "gy", split_axis=0, concat_axis=0, tiled=True)
+        [whole(both), whole((C, 2 * modes))],
+        whole((2 * C, 2 * modes)),
+        shape((2 * C, 2 * modes), BF16),
+    )(where, arrived, grad_spectrum)
+    other = lax.ppermute(spectra, "dp", [(0, 1), (1, 0)])
     grad_spec = call(
         weight_grads,
-        "weight_grads",
         1,
-        [whole(spectrum.shape), whole(other.shape)],
+        [whole(spectra.shape), whole(spectra.shape)],
         whole((2, modes, C * C)),
         shape((2, modes, C * C), F32),
-    )(where, spectrum, other)
+    )(where, spectra, other)
     grad_fields = call(
         inverse_yz,
-        "inverse_yz",
-        groups,
-        [
-            whole(gathered.shape),
-            columns,
-            whole(z_table.shape),
-            at_gy(y_table.shape),
-            whole(point_weight.shape),
-        ],
+        steps,
+        [whole(y_pieces), columns] + tables + [whole(point_weight.shape)],
         columns,
         shape((rows, local_yz), BF16),
-        [pltpu.VMEM((2 * MZ, local_y, rows), F32), pltpu.VMEM((rows, rows), BF16)],
+        [lines, pltpu.VMEM((rows, rows), BF16)],
     )(where, gathered, grad_pre, z_table, y_table, point_weight)
     return grad_fields.reshape(fields.shape), grad_spec.reshape(spec_weight.shape)
 
@@ -337,6 +413,7 @@
         P(None, "gx", None, "gy", None),
         P(),
     )
+
     return jax.shard_map(
         on_device,
         mesh=mesh,

time: 95.6 us -> 105 us (1.098)
  starting transfers between devices: 21.9 us -> 35.8 us
  waiting for transfers between devices: 13 us -> 5.4 us
  Pallas kernels: 14 us -> 21.5 us
  local copies, waits for them, and re-layouts: 6.45 us -> 1.7 us
    ppermute x1 -> x5, starting transfers between devices: 5.31 us -> 18.4 us  [the longest x3 9 us: on_device(): lax.ppermute(field_lines[k], 'gy', [(i, (i + 2 * k) % count_y) for i in r...]
    all_to_all x2, waiting for transfers between devices: 9.61 us -> 0.01 us  [exchange(): return lax.all_to_all(pieces, axis, split_axis=0, concat_axis=0, tiled=True)]
    pallas_call x6 -> x10, Pallas kernels: 14 us -> 21.5 us  [the longest x1 5.65 us: on_device(): call(forward_fields, steps, [columns] + tables, (whole(half), whole(half)...]
    unnamed x20 -> x18, local copies, waits for them, and re-layouts: 5.69 us -> 0.94 us
    ppermute x1 -> x5, waiting for transfers between devices: 3.37 us -> 5.4 us  [the longest x1 2.72 us: on_device(): other = lax.ppermute(spectra, 'dp', [(0, 1), (1, 0)])]
  transfers between devices with their start and end apart: 3 -> 7, of which waited for: 2 -> 3; matrix products, arithmetic and copies ran while one was open for 1% -> 1% of each run, Pallas kernels for 1% -> 8%
where the time goes in v2:
time: 105 us; the launch traced here: 104 us
  blocking collectives  37.9 us (36%)
  starting transfers between devices  35.8 us (34%)
  Pallas kernels  21.5 us (20%)
  waiting for transfers between devices  5.4 us (5%)
  local copies, waits for them, and re-layouts  1.7 us (2%)
    all_to_all x2, blocking collectives, exchange(): return lax.all_to_all(pieces, axis, split_axis=0, concat_axis=0, tiled=True)  37.9 us
    all_to_all x2, starting transfers between devices, exchange(): return lax.all_to_all(pieces, axis, split_axis=0, concat_axis=0, tiled=True)  17.5 us
    ppermute x3, starting transfers between devices, on_device(): lax.ppermute(field_lines[k], 'gy', [(i, (i + 2 * k) % count_y) for i in r...  9 us
    ppermute x1, starting transfers between devices, on_device(): other = lax.ppermute(spectra, 'dp', [(0, 1), (1, 0)])  6.02 us
    pallas_call x1, Pallas kernels, on_device(): call(forward_fields, steps, [columns] + tables, (whole(half), whole(half)...  5.65 us
    pallas_call x1, Pallas kernels, on_device(): call(forward_grads, steps, [columns, columns] + tables, (columns, whole(y...  5.61 us
    pallas_call x1, Pallas kernels, on_device(): call(inverse_yz, steps, [whole(y_pieces), columns] + tables + [whole(poin...  3.44 us
    ppermute x1, starting transfers between devices, on_device(): taken = lax.ppermute(given, 'gy', [(i, i ^ 1) for i in range(count_y)])  3.33 us
  transfers between devices with their start and end apart: 7, of which 3 were waited for; matrix products, arithmetic and copies ran while one was open for 1% of the time, Pallas kernels for 8%

profile of v2, /device:TPU:1, one launch (start us, length us, event | category | flops | bytes accessed | tf_op | source)
XLA Modules:
  0.0 103.8 jit_solution(12698721515967381084)
XLA Ops:
  0.6 0.7 pad_add_fusion.where
  1.3 5.6 %shard_map.95 = (bf16[128,4096]{1,0:T(8,128)(2,1)}, bf16[8,128,128]{2,1,0:T(8,128)(2,1)}) custom-call(s32[2]{0:T(128)} %pad_add_fusion.where, bf16[128,4096]{1,0:T(8,128)(2,1)} %bitcast.7, bf16[128,4096]{1,0:T(8,128)(2,1)} %bitcast.8, bf16[256,512]{1,0:T(8,128)(2,1)} %constant.15.clone.z_table, bf16[8,128,256]{2,1,0:T(8,128)(2,1)} %constant.16.clone.y_table), custom_call_target="tpu_custom_call" | custom-call | tf_op jit(solution)/shard_map/pallas_call | solution.py:317
  6.9 0.0 copy-start
  6.9 0.0 copy-start.5
  6.9 19.0 %all_to_all.20.arrived = bf16[8,128,128]{2,1,0:T(8,128)(2,1)S(1)} all-to-all(bf16[8,128,128]{2,1,0:T(8,128)(2,1)} %get-tuple-element.12), channel_id=1, replica_groups=mesh['dp'=2,'gx'=32,'gy'=8] {'gy'}, dimensions={0} | all-to-all | bytes 524288 | tf_op jit(solution)/shard_map/all_to_all | solution.py:294
  25.9 0.0 copy-done
  25.9 0.0 copy-done.5
  25.9 1.4 %shard_map.96 = bf16[32,16,128]{2,1,0:T(8,128)(2,1)} custom-call(s32[2]{0:T(128)S(1)} %copy-done.5, bf16[8,128,128]{2,1,0:T(8,128)(2,1)S(1)} %all_to_all.20.arrived, bf16[32,2,32,128]{3,2,1,0:T(8,128)(2,1)S(1)} %copy-done), custom_call_target="tpu_custom_call" | custom-call | tf_op jit(solution)/shard_map/pallas_call | solution.py:365
  27.3 9.1 %all-to-all-start.1 = ((bf16[32,16,128]{2,1,0:T(8,128)(2,1)}), bf16[32,16,128]{2,1,0:T(8,128)(2,1)S(1)}, u32[]{:S(2)}, u32[]{:S(2)}) async-start(bf16[32,16,128]{2,1,0:T(8,128)(2,1)} %shard_map.96), calls=%async_computation.1 | async-start | bytes 262144 | tf_op jit(solution)/shard_map/all_to_all | solution.py:294
  36.4 5.7 %shard_map.97 = (bf16[4,128,128]{2,1,0:T(8,128)(2,1)}, bf16[4,128,128]{2,1,0:T(8,128)(2,1)}) custom-call(s32[2]{0:T(128)} %pad_add_fusion.where, bf16[128,4096]{1,0:T(8,128)(2,1)} %bitcast.9, bf16[256,512]{1,0:T(8,128)(2,1)} %constant.15.clone.z_table, bf16[8,128,256]{2,1,0:T(8,128)(2,1)} %constant.16.clone.y_table), custom_call_target="tpu_custom_call" | custom-call | tf_op jit(solution)/shard_map/pallas_call | solution.py:335
  42.1 0.0 copy-start.6
  42.1 3.3 %collective-permute-start = (bf16[4,128,128]{2,1,0:T(8,128)(2,1)}, bf16[4,128,128]{2,1,0:T(8,128)(2,1)S(1)}, u32[]{:S(2)}, u32[]{:S(2)}) collective-permute-start(bf16[4,128,128]{2,1,0:T(8,128)(2,1)} %get-tuple-element.14), channel_id=1, source_target_pairs={{0,1},{1,0},{2,3},{3,2},{4,5},{5,4},{6,7},{7,6},{8,9},{9,8},{10,11... | collective-permute-start | bytes 393224 | tf_op jit(solution)/shard_map/ppermute | solution.py:344
  45.4 1.2 %collective-permute-done.taken = bf16[4,128,128]{2,1,0:T(8,128)(2,1)S(1)} collective-permute-done((bf16[4,128,128]{2,1,0:T(8,128)(2,1)}, bf16[4,128,128]{2,1,0:T(8,128)(2,1)S(1)}, u32[]{:S(2)}, u32[]{:S(2)}) %collective-permute-start) | collective-permute-done | bytes 131104 | tf_op jit(solution)/shard_map/ppermute | solution.py:344
  46.6 0.0 copy-done.6
  46.6 0.0 copy-start.4
  46.6 0.9 copy-done.4
  47.5 0.0 copy-start.8
  47.5 0.6 shard_map.98
  48.1 1.9 %collective-permute-start.1 = (bf16[128,128]{1,0:T(8,128)(2,1)S(1)}, bf16[128,128]{1,0:T(8,128)(2,1)S(1)}, u32[]{:S(2)}, u32[]{:S(2)}) collective-permute-start(bf16[128,128]{1,0:T(8,128)(2,1)S(1)} %get-tuple-element.16), channel_id=1, source_target_pairs={{0,2},{1,3},{2,4},{3,5},{4,6},{5,7},{6,0},{7,1},{8,10},{9,11},{10,... | collective-permute-start | bytes 98312 | tf_op jit(solution)/shard_map/ppermute | solution.py:353
  50.0 3.2 %collective-permute-start.2 = (bf16[128,128]{1,0:T(8,128)(2,1)S(1)}, bf16[128,128]{1,0:T(8,128)(2,1)S(1)}, u32[]{:S(2)}, u32[]{:S(2)}) collective-permute-start(bf16[128,128]{1,0:T(8,128)(2,1)S(1)} %get-tuple-element.17), channel_id=1, source_target_pairs={{0,4},{1,5},{2,6},{3,7},{4,0},{5,1},{6,2},{7,3},{8,12},{9,13},{10,... | collective-permute-start | bytes 98312 | tf_op jit(solution)/shard_map/ppermute | solution.py:353
  53.2 3.9 %collective-permute-start.3 = (bf16[128,128]{1,0:T(8,128)(2,1)S(1)}, bf16[128,128]{1,0:T(8,128)(2,1)S(1)}, u32[]{:S(2)}, u32[]{:S(2)}) collective-permute-start(bf16[128,128]{1,0:T(8,128)(2,1)S(1)} %get-tuple-element.18), channel_id=1, source_target_pairs={{0,6},{1,7},{2,0},{3,1},{4,2},{5,3},{6,4},{7,5},{8,14},{9,15},{10,... | collective-permute-start | bytes 98312 | tf_op jit(solution)/shard_map/ppermute | solution.py:353
  57.1 0.0 copy-done.8
  57.2 0.0 collective-permute-done.1.refs_1_
  57.2 0.0 collective-permute-done.2.refs_2_
  57.2 1.5 %collective-permute-done.3.refs_3_ = bf16[128,128]{1,0:T(8,128)(2,1)S(1)} collective-permute-done((bf16[128,128]{1,0:T(8,128)(2,1)S(1)}, bf16[128,128]{1,0:T(8,128)(2,1)S(1)}, u32[]{:S(2)}, u32[]{:S(2)}) %collective-permute-start.3) | collective-permute-done | bytes 32800 | tf_op jit(solution)/shard_map/ppermute | solution.py:353
  58.7 0.8 shard_map.99.fields
  59.5 0.0 all-to-all-done.1.arrived
  59.5 1.0 shard_map.100
  60.5 19.0 %all_to_all.21.arrived = bf16[32,32,128]{2,1,0:T(8,128)(2,1)S(1)} all-to-all(bf16[32,32,128]{2,1,0:T(8,128)(2,1)S(1)} %get-tuple-element.19), channel_id=1, replica_groups=mesh['dp'=2,'gx'=32,'gy'=8] {'gx'}, dimensions={0} | all-to-all | bytes 524288 | tf_op jit(solution)/shard_map/all_to_all | solution.py:294
  79.5 0.0 copy-start.3
  79.5 1.6 %shard_map.101 = bf16[8,128,128]{2,1,0:T(8,128)(2,1)} custom-call(s32[2]{0:T(128)S(1)} %copy-done.6, bf16[32,32,128]{2,1,0:T(8,128)(2,1)S(1)} %all_to_all.21.arrived, bf16[32,2,32,128]{3,2,1,0:T(8,128)(2,1)S(1)} %copy-done), custom_call_target="tpu_custom_call" | custom-call | tf_op jit(solution)/shard_map/pallas_call | solution.py:378
  81.1 0.0 copy-start.1
  81.1 8.4 %all-to-all-start.3 = ((bf16[8,128,128]{2,1,0:T(8,128)(2,1)}), bf16[8,128,128]{2,1,0:T(8,128)(2,1)S(1)}, u32[]{:S(2)}, u32[]{:S(2)}) async-start(bf16[8,128,128]{2,1,0:T(8,128)(2,1)} %shard_map.101), calls=%async_computation.3 | async-start | bytes 524288 | tf_op jit(solution)/shard_map/all_to_all | solution.py:294
  89.4 0.6 shard_map.103.own
  90.0 0.0 copy-start.2
  90.0 6.0 %collective-permute-start.4 = (bf16[32,128]{1,0:T(8,128)(2,1)S(1)}, bf16[32,128]{1,0:T(8,128)(2,1)S(1)}, u32[]{:S(2)}, u32[]{:S(2)}) collective-permute-start(bf16[32,128]{1,0:T(8,128)(2,1)S(1)} %shard_map.103.own), channel_id=1, source_target_pairs={{0,256},{256,0},{1,257},{257,1},{2,258},{258,2},{3,259},{259,3},{4... | collective-permute-start | bytes 24584 | tf_op jit(solution)/shard_map/ppermute | solution.py:389
  96.1 2.7 %collective-permute-done.4.other = bf16[32,128]{1,0:T(8,128)(2,1)S(1)} collective-permute-done((bf16[32,128]{1,0:T(8,128)(2,1)S(1)}, bf16[32,128]{1,0:T(8,128)(2,1)S(1)}, u32[]{:S(2)}, u32[]{:S(2)}) %collective-permute-start.4) | collective-permute-done | bytes 8224 | tf_op jit(solution)/shard_map/ppermute | solution.py:389
  98.8 0.8 shard_map.104
  99.6 0.0 copy-start.7
  99.6 0.7 reshape.27
  100.3 0.0 all-to-all-done.3.arrived
  100.3 0.0 copy-done.3
  100.3 0.0 copy-done.1
  100.3 0.0 copy-done.2
  100.4 0.0 copy-done.7
  100.4 3.4 %shard_map.102 = bf16[128,4096]{1,0:T(8,128)(2,1)} custom-call(s32[2]{0:T(128)S(1)} %copy-done.6, bf16[8,128,128]{2,1,0:T(8,128)(2,1)S(1)} %all-to-all-done.3.arrived, bf16[128,4096]{1,0:T(8,128)(2,1)S(1)} %copy-done.3, bf16[256,512]{1,0:T(8,128)(2,1)S(1)} %copy-done.2, bf16[8,128,256]{2,1,0:T(8,128)(2,1)S(1)} %copy-done.1, bf16[16,16]{1,0:T(8,128)(2,1)S(1)} %copy-done.7), custom_call_target="tpu_custom_call" | custom-call | tf_op jit(solution)/shard_map/pallas_call | solution.py:397
  (1 shorter events, 0.0 us)
Async XLA Ops:
  6.9 19.0 %copy-start = (bf16[32,2,32,128]{3,2,1,0:T(8,128)(2,1)S(1)}, bf16[32,2,32,128]{3,2,1,0:T(8,128)(2,1)}, u32[]{:S(2)}) copy-start(bf16[32,2,32,128]{3,2,1,0:T(8,128)(2,1)} %constant.17.clone.x_rows.refs_4_) | copy-start | bytes 1572868
  6.9 19.0 %copy-start.5 = (s32[2]{0:T(128)S(1)}, s32[2]{0:T(128)}, u32[]{:S(2)}) copy-start(s32[2]{0:T(128)} %pad_add_fusion.where) | copy-start | bytes 28
  27.3 32.2 %all-to-all-start.1 = ((bf16[32,16,128]{2,1,0:T(8,128)(2,1)}), bf16[32,16,128]{2,1,0:T(8,128)(2,1)S(1)}, u32[]{:S(2)}, u32[]{:S(2)}) async-start(bf16[32,16,128]{2,1,0:T(8,128)(2,1)} %shard_map.96), calls=%async_computation.1 | async-start | bytes 262144 | tf_op jit(solution)/shard_map/all_to_all | solution.py:294
  42.1 4.5 %copy-start.6 = (s32[2]{0:T(128)S(1)}, s32[2]{0:T(128)}, u32[]{:S(2)}) copy-start(s32[2]{0:T(128)} %pad_add_fusion.where) | copy-start | bytes 28
  42.1 4.5 %collective-permute-start = (bf16[4,128,128]{2,1,0:T(8,128)(2,1)}, bf16[4,128,128]{2,1,0:T(8,128)(2,1)S(1)}, u32[]{:S(2)}, u32[]{:S(2)}) collective-permute-start(bf16[4,128,128]{2,1,0:T(8,128)(2,1)} %get-tuple-element.14), channel_id=1, source_target_pairs={{0,1},{1,0},{2,3},{3,2},{4,5},{5,4},{6,7},{7,6},{8,9},{9,8},{10,11... | collective-permute-start | bytes 393224 | tf_op jit(solution)/shard_map/ppermute | solution.py:344
  46.6 0.9 copy-start.4
  47.5 9.6 %copy-start.8 = (bf16[2,1,32,2,256]{4,3,2,1,0:T(2,128)(2,1)S(1)}, bf16[2,1,32,2,256]{4,3,2,1,0:T(2,128)(2,1)}, u32[]{:S(2)}) copy-start(bf16[2,1,32,2,256]{4,3,2,1,0:T(2,128)(2,1)} %param.11) | copy-start | bytes 196612
  48.1 9.1 %collective-permute-start.1 = (bf16[128,128]{1,0:T(8,128)(2,1)S(1)}, bf16[128,128]{1,0:T(8,128)(2,1)S(1)}, u32[]{:S(2)}, u32[]{:S(2)}) collective-permute-start(bf16[128,128]{1,0:T(8,128)(2,1)S(1)} %get-tuple-element.16), channel_id=1, source_target_pairs={{0,2},{1,3},{2,4},{3,5},{4,6},{5,7},{6,0},{7,1},{8,10},{9,11},{10,... | collective-permute-start | bytes 98312 | tf_op jit(solution)/shard_map/ppermute | solution.py:353
  50.0 7.2 %collective-permute-start.2 = (bf16[128,128]{1,0:T(8,128)(2,1)S(1)}, bf16[128,128]{1,0:T(8,128)(2,1)S(1)}, u32[]{:S(2)}, u32[]{:S(2)}) collective-permute-start(bf16[128,128]{1,0:T(8,128)(2,1)S(1)} %get-tuple-element.17), channel_id=1, source_target_pairs={{0,4},{1,5},{2,6},{3,7},{4,0},{5,1},{6,2},{7,3},{8,12},{9,13},{10,... | collective-permute-start | bytes 98312 | tf_op jit(solution)/shard_map/ppermute | solution.py:353
  53.2 5.5 %collective-permute-start.3 = (bf16[128,128]{1,0:T(8,128)(2,1)S(1)}, bf16[128,128]{1,0:T(8,128)(2,1)S(1)}, u32[]{:S(2)}, u32[]{:S(2)}) collective-permute-start(bf16[128,128]{1,0:T(8,128)(2,1)S(1)} %get-tuple-element.18), channel_id=1, source_target_pairs={{0,6},{1,7},{2,0},{3,1},{4,2},{5,3},{6,4},{7,5},{8,14},{9,15},{10,... | collective-permute-start | bytes 98312 | tf_op jit(solution)/shard_map/ppermute | solution.py:353
  79.5 20.9 %copy-start.3 = (bf16[128,4096]{1,0:T(8,128)(2,1)S(1)}, bf16[128,4096]{1,0:T(8,128)(2,1)}, u32[]{:S(2)}) copy-start(bf16[128,4096]{1,0:T(8,128)(2,1)} %get-tuple-element.20.grad_pre) | copy-start | bytes 3145732
  81.1 19.3 %copy-start.1 = (bf16[8,128,256]{2,1,0:T(8,128)(2,1)S(1)}, bf16[8,128,256]{2,1,0:T(8,128)(2,1)}, u32[]{:S(2)}) copy-start(bf16[8,128,256]{2,1,0:T(8,128)(2,1)} %constant.16.clone.y_table) | copy-start | bytes 1572868
  81.1 19.2 %all-to-all-start.3 = ((bf16[8,128,128]{2,1,0:T(8,128)(2,1)}), bf16[8,128,128]{2,1,0:T(8,128)(2,1)S(1)}, u32[]{:S(2)}, u32[]{:S(2)}) async-start(bf16[8,128,128]{2,1,0:T(8,128)(2,1)} %shard_map.101), calls=%async_computation.3 | async-start | bytes 524288 | tf_op jit(solution)/shard_map/all_to_all | solution.py:294
  90.0 10.3 %copy-start.2 = (bf16[256,512]{1,0:T(8,128)(2,1)S(1)}, bf16[256,512]{1,0:T(8,128)(2,1)}, u32[]{:S(2)}) copy-start(bf16[256,512]{1,0:T(8,128)(2,1)} %constant.15.clone.z_table) | copy-start | bytes 786436
  90.0 8.8 %collective-permute-start.4 = (bf16[32,128]{1,0:T(8,128)(2,1)S(1)}, bf16[32,128]{1,0:T(8,128)(2,1)S(1)}, u32[]{:S(2)}, u32[]{:S(2)}) collective-permute-start(bf16[32,128]{1,0:T(8,128)(2,1)S(1)} %shard_map.103.own), channel_id=1, source_target_pairs={{0,256},{256,0},{1,257},{257,1},{2,258},{258,2},{3,259},{259,3},{4... | collective-permute-start | bytes 24584 | tf_op jit(solution)/shard_map/ppermute | solution.py:389
  99.6 0.8 copy-start.7

commit v3 on v1

v3 whole, which is shorter than its diff:
```python
import math

import jax
import jax.numpy as jnp
import numpy as np
from jax import lax
from jax.experimental import pallas as pl
from jax.experimental.pallas import tpu as pltpu
from jax.sharding import PartitionSpec as P

C = 16
NX = 256
NY = 512
NZ = 64
MX = 32
MY = 32
MZ = 16
GROUP = 8

F32 = jnp.float32
BF16 = jnp.bfloat16
HIGHEST = lax.Precision.HIGHEST


def signed_freqs(kept, length):
    index = np.arange(kept)
    return np.where(index < kept // 2, index, length - kept + index)


def cos_sin(freqs, points, length):
    turns = points[:, None] * freqs[None, :] % length
    angle = turns.astype(np.float32) * np.float32(2.0 * math.pi / length)
    return np.cos(angle).astype(np.float32), np.sin(angle).astype(np.float32)


def z_block_table():
    cosine, sine = cos_sin(np.arange(MZ), np.arange(NZ), NZ)
    parts = np.stack([cosine.T, -sine.T], axis=1)
    same = np.eye(GROUP, dtype=np.float32)
    table = parts[:, :, None, None, :] * same[None, None, :, :, None]
    return table.reshape(2 * MZ * GROUP, GROUP * NZ).astype(BF16)


def y_block_tables(count, local_y, local_mz):
    cosine, sine = cos_sin(signed_freqs(MY, NY), np.arange(NY), NY)
    upper = np.stack([cosine, sine], axis=-1)
    lower = np.stack([-sine, cosine], axis=-1)
    table = np.stack([upper, lower], axis=0)
    table = table.reshape(2, count, local_y, MY, 2).transpose(1, 0, 3, 4, 2)
    same = np.eye(local_mz, dtype=np.float32)
    table = table[:, :, :, None, None, :, :] * same[None, None, None, :, :, None, None]
    return table.reshape(count, 2 * MY * local_mz, local_mz * 2 * local_y).astype(BF16)


def x_row_tables(count, local_x):
    cosine, sine = cos_sin(signed_freqs(MX, NX), np.arange(NX), NX)
    table = np.stack([cosine, sine], axis=0).reshape(2, count, local_x, MX)
    table = table.transpose(1, 0, 3, 2)
    return np.tile(table, (1, 1, 1, 128 // local_x)).astype(BF16)


def dot(left, right, dims, precision=None):
    return lax.dot_general(
        left, right, (dims, ((), ())), preferred_element_type=F32, precision=precision
    )


def gelu_slope(value):
    cdf = 0.5 * (1.0 + lax.erf(value * (1.0 / math.sqrt(2.0))))
    return cdf + value * jnp.exp(-0.5 * value * value) * (1.0 / math.sqrt(2.0 * math.pi))


def copies_in(sources, targets, sems, groups):
    width = targets[0].shape[1] // groups
    copies = []
    for group in range(groups):
        lanes = pl.ds(group * width, width)
        copies.append(
            [
                pltpu.make_async_copy(
                    source.at[:, lanes], target.at[:, lanes], sems.at[index, group]
                )
                for index, (source, target) in enumerate(zip(sources, targets))
            ]
        )
    return copies


def forward_zy(
    fields, pre_act, cotangent, z_source, y_source, grad_pre, pieces,
    fields_in, pre_in, cotangent_in, z_table, y_table, lines, sems, table_sems,
):
    groups = sems.shape[1]
    tables = [
        pltpu.make_async_copy(z_source, z_table, table_sems.at[0]),
        pltpu.make_async_copy(y_source.at[lax.axis_index("gy")], y_table, table_sems.at[1]),
    ]
    copies = copies_in(
        (pre_act, cotangent, fields), (pre_in, cotangent_in, fields_in), sems, groups
    )
    for copy in copies[0] + tables[:1]:
        copy.start()
    for group in copies[1:]:
        for copy in group:
            copy.start()
    tables[1].start()
    width = pre_in.shape[1] // groups
    pair = []
    for group, arrived in enumerate(copies):
        for copy in arrived:
            copy.wait()
        part = slice(group * width, (group + 1) * width)
        slope = gelu_slope(pre_in[:, part].astype(F32))
        grad = (cotangent_in[:, part].astype(F32) * slope).astype(BF16)
        grad_pre[:, part] = grad
        both = jnp.concatenate([fields_in[:, part], grad], axis=0)
        if group == 0:
            tables[0].wait()
        spectra = dot(z_table[...], both, ((1,), (1,)))
        pair.append(spectra.reshape(2 * MZ, GROUP, both.shape[0]))
        if len(pair) == 2:
            rows = slice((group - 1) * GROUP, (group + 1) * GROUP)
            lines[:, rows, :] = jnp.concatenate(pair, axis=1).astype(BF16)
            pair = []
    tables[1].wait()
    count = pieces.shape[0]
    per = 2 * MZ // count
    for index in range(count):
        block = lines[index * per : (index + 1) * per]
        block = block.reshape(per * block.shape[1], block.shape[2])
        pieces[index] = dot(y_table[...], block, ((1,), (0,))).astype(BF16)


def add_up(arrived):
    total = arrived[0].astype(F32)
    for index in range(1, arrived.shape[0]):
        total = total + arrived[index].astype(F32)
    return total


def x_blocks(x_rows):
    lanes = x_rows.shape[3]
    owner = lax.broadcasted_iota(jnp.int32, (C, lanes), 1) // (lanes // C)
    mask = owner == lax.broadcasted_iota(jnp.int32, (C, lanes), 0)
    rows = x_rows[lax.axis_index("gx")].astype(F32)
    blocks = []
    for part in range(2):
        table = jnp.where(mask[None], rows[part][:, None, :], 0.0)
        blocks.append(table.reshape(MX * C, lanes).astype(BF16))
    return blocks


def forward_x(arrived, x_rows, pieces):
    blocks = x_blocks(x_rows)
    total = add_up(arrived)
    half = total.shape[0] // 2
    swapped = jnp.concatenate([total[half:], -total[:half]], axis=0).astype(BF16)
    total = total.astype(BF16)
    lanes = blocks[0].shape[1]
    for part in range(2):
        own = slice(part * lanes, (part + 1) * lanes)
        spectra = dot(blocks[0], total[:, own], ((1,), (1,)))
        spectra = spectra + dot(blocks[1], swapped[:, own], ((1,), (1,)))
        spectra = spectra.reshape(MX, C, spectra.shape[1]).astype(BF16)
        pieces[:, part * C : (part + 1) * C, :] = spectra


def mode_scale(rows, local_mz):
    line = lax.broadcasted_iota(jnp.int32, (rows, 1), 0) % local_mz
    line = line + lax.axis_index("gy") * local_mz
    return jnp.where(line == 0, 1.0, 2.0).astype(F32) / float(NX * NY * NZ)


def repeat_tables():
    lane = lax.broadcasted_iota(jnp.int32, (C, C * C), 1)
    row = lax.broadcasted_iota(jnp.int32, (C, C * C), 0)
    outer = (lane // C == row).astype(F32)
    inner = (lane % C == row).astype(F32)
    return outer, inner


def mode_products(arrived, weights, spectrum, grad_hat):
    total = add_up(arrived).astype(BF16)
    spectrum[...] = total
    modes = total.shape[1] // 2
    outer, inner = repeat_tables()
    grads = dot(total[C:], inner.astype(BF16), ((0,), (0,)))
    scale = mode_scale(modes, modes // MY)
    real_d = grads[:modes] * scale
    imag_d = grads[modes:] * scale
    real_w = weights[0, 0].astype(F32).reshape(modes, C * C)
    imag_w = weights[1, 0].astype(F32).reshape(modes, C * C)
    products = jnp.concatenate(
        [real_w * real_d + imag_w * imag_d, real_w * imag_d - imag_w * real_d], axis=0
    )
    values = dot(outer, products, ((1,), (1,)), HIGHEST).astype(BF16)
    grad_hat[...] = jnp.broadcast_to(values[None], grad_hat.shape)


def weight_grads(own, other, result):
    modes = own.shape[1] // 2
    outer, inner = repeat_tables()
    outer = outer.astype(BF16)
    inner = inner.astype(BF16)
    scale = mode_scale(modes, modes // MY)
    real_sum = jnp.zeros((modes, C * C), F32)
    imag_sum = jnp.zeros((modes, C * C), F32)
    for spectrum in (own, other):
        values = spectrum[...]
        field = dot(values[:C], outer, ((0,), (0,)))
        grads = dot(values[C:], inner, ((0,), (0,)))
        real_u, imag_u = field[:modes], field[modes:]
        real_d, imag_d = grads[:modes] * scale, grads[modes:] * scale
        real_sum = real_sum + (real_u * real_d + imag_u * imag_d)
        imag_sum = imag_sum + (real_u * imag_d - imag_u * real_d)
    for part, total in enumerate((real_sum, imag_sum)):
        result[part, 0] = total.reshape(result.shape[2:])


def inverse_x(arrived, x_rows, result):
    blocks = x_blocks(x_rows)
    values = arrived[...].reshape(MX * C, arrived.shape[2])
    half = values.shape[1] // 2
    swapped = jnp.concatenate([-values[:, half:], values[:, :half]], axis=1)
    sums = dot(values, blocks[0], ((0,), (0,))) + dot(swapped, blocks[1], ((0,), (0,)))
    result[...] = jnp.broadcast_to(sums.astype(BF16)[None], result.shape)


def inverse_yz(
    arrived, grad_pre, z_table, y_tables, point, result, lines, staged, sems
):
    y_table = y_tables[lax.axis_index("gy")]
    rows = staged.shape[0]
    local_x = rows // C
    row = lax.broadcasted_iota(jnp.int32, (rows, C), 0) // local_x
    pick = (row == lax.broadcasted_iota(jnp.int32, (rows, C), 1)).astype(BF16)
    spread = dot(pick, point[...], ((1,), (0,))).astype(BF16)
    spread = dot(spread, pick, ((1,), (1,)))
    left = lax.broadcasted_iota(jnp.int32, (rows, rows), 0) % local_x
    right = lax.broadcasted_iota(jnp.int32, (rows, rows), 1) % local_x
    mixing = jnp.where(left == right, spread, 0.0).astype(BF16)
    count = arrived.shape[0]
    per = 2 * MZ // count
    for index in range(count):
        block = dot(y_table, arrived[index], ((0,), (0,)))
        lines[index * per : (index + 1) * per] = block.reshape(per, -1, rows)
    width = z_table.shape[1]
    copies = []
    for group in range(result.shape[1] // width):
        block = lines[:, group * GROUP : (group + 1) * GROUP, :]
        block = block.reshape(2 * MZ * GROUP, rows).astype(BF16)
        spectral = dot(block, z_table[...], ((0,), (0,)))
        part = slice(group * width, (group + 1) * width)
        mixed = dot(mixing, grad_pre[:, part], ((1,), (0,)))
        staged[:, part] = (spectral + mixed).astype(BF16)
        copy = pltpu.make_async_copy(
            staged.at[:, pl.ds(group * width, width)],
            result.at[:, pl.ds(group * width, width)],
            sems.at[group],
        )
        copy.start()
        copies.append(copy)
    for copy in copies:
        copy.wait()


VMEM = pl.BlockSpec(memory_space=pltpu.VMEM)
HBM = pl.BlockSpec(memory_space=pltpu.HBM)


def call(body, ins, outs, scratch=(), vmem=24):
    values = [
        pltpu.with_memory_space_constraint(value, spec.memory_space) for value, spec in ins
    ]
    specs = [spec for _, spec in ins]
    shapes = [
        pltpu.VMEM(shape, dtype) if spec is VMEM else jax.ShapeDtypeStruct(shape, dtype)
        for shape, dtype, spec in outs
    ]
    return pl.pallas_call(
        body,
        in_specs=specs,
        out_specs=[spec for _, _, spec in outs],
        out_shape=shapes,
        scratch_shapes=list(scratch),
        compiler_params=pltpu.CompilerParams(vmem_limit_bytes=vmem << 20),
    )(*values)


def exchange(pieces, axis):
    return lax.all_to_all(pieces, axis, split_axis=0, concat_axis=0, tiled=True)


def on_device(fields, pre_act, cotangent, spec_weight, point_weight):
    count_x = lax.axis_size("gx")
    count_y = lax.axis_size("gy")
    _, channels, local_x, local_yz = fields.shape
    local_y = local_yz // NZ
    local_mz = spec_weight.shape[3]
    rows = channels * local_x
    modes = MY * local_mz
    groups = local_y // GROUP
    z_table = jnp.asarray(z_block_table())
    y_table = jnp.asarray(y_block_tables(count_y, local_y, local_mz))
    x_rows = jnp.asarray(x_row_tables(count_x, local_x))
    whole = (rows, local_yz)
    dma = pltpu.SemaphoreType.DMA

    grad_pre, pieces = call(
        forward_zy,
        [
            (fields.reshape(whole), HBM),
            (pre_act.reshape(whole), HBM),
            (cotangent.reshape(whole), HBM),
            (z_table, HBM),
            (y_table, HBM),
        ],
        [(whole, BF16, VMEM), ((count_y, 2 * modes, 2 * rows), BF16, VMEM)],
        [pltpu.VMEM(whole, BF16)] * 3
        + [
            pltpu.VMEM(z_table.shape, BF16),
            pltpu.VMEM(y_table.shape[1:], BF16),
            pltpu.VMEM((2 * MZ, local_y, 2 * rows), BF16),
            dma((3, groups)),
            dma((2,)),
        ],
    )
    arrived = exchange(pieces, "gy")
    (pieces,) = call(
        forward_x,
        [(arrived, VMEM), (x_rows, VMEM)],
        [((count_x, 2 * C, 2 * modes), BF16, VMEM)],
    )
    arrived = exchange(pieces, "gx")
    spectrum, pieces = call(
        mode_products,
        [(arrived, VMEM), (spec_weight, VMEM)],
        [((2 * C, 2 * modes), BF16, VMEM), ((count_x, C, 2 * modes), BF16, VMEM)],
    )
    arrived = exchange(pieces, "gx")
    other = lax.ppermute(spectrum, "dp", [(0, 1), (1, 0)])
    (grad_spec,) = call(
        weight_grads,
        [(spectrum, VMEM), (other, VMEM)],
        [(spec_weight.shape, F32, pl.BlockSpec())],
    )
    (pieces,) = call(
        inverse_x,
        [(arrived, VMEM), (x_rows, VMEM)],
        [((count_y, 2 * modes, rows), BF16, VMEM)],
    )
    arrived = exchange(pieces, "gy")
    (grad_fields,) = call(
        inverse_yz,
        [
            (arrived, VMEM),
            (grad_pre, VMEM),
            (z_table, VMEM),
            (y_table, VMEM),
            (point_weight, VMEM),
        ],
        [(whole, BF16, HBM)],
        [
            pltpu.VMEM((2 * MZ, local_y, rows), F32),
            pltpu.VMEM(whole, BF16),
            dma((groups,)),
        ],
    )
    return grad_fields.reshape(fields.shape), grad_spec


def solution(mesh):
    placed = (
        P("dp", None, "gx", "gy"),
        P("dp", None, "gx", "gy"),
        P("dp", None, "gx", "gy"),
        P(None, "gx", None, "gy", None),
        P(),
    )

    return jax.shard_map(
        on_device,
        mesh=mesh,
        in_specs=placed,
        out_specs=(P("dp", None, "gx", "gy"), P(None, "gx", None, "gy", None)),
        check_vma=False,
    )
```

time: 95.6 us -> 84.5 us (0.88)
  blocking collectives: 38.7 us -> 58.1 us
  starting transfers between devices: 21.9 us -> 11.9 us
  waiting for transfers between devices: 13 us -> 3.51 us
  local copies, waits for them, and re-layouts: 6.45 us -> 0.02 us
  Pallas kernels: 14 us -> 9.85 us
    all_to_all x2 -> x3, blocking collectives: 38.7 us -> 58.1 us  [exchange(): return lax.all_to_all(pieces, axis, split_axis=0, concat_axis=0, tiled=True)]
    all_to_all x2 -> x1, starting transfers between devices: 16.6 us -> 6.69 us  [exchange(): return lax.all_to_all(pieces, axis, split_axis=0, concat_axis=0, tiled=True)]
    all_to_all x2 -> x1, waiting for transfers between devices: 9.61 us -> 0.01 us  [exchange(): return lax.all_to_all(pieces, axis, split_axis=0, concat_axis=0, tiled=True)]
    unnamed x20 -> x10, local copies, waits for them, and re-layouts: 5.69 us -> 0.02 us
    pallas_call x6, Pallas kernels: 14 us -> 9.85 us  [call(): pl.pallas_call(body, in_specs=specs, out_specs=[spec for _, _, spec in ou...]
  transfers between devices with their start and end apart: 3 -> 2, of which waited for: 2 -> 1; matrix products, arithmetic and copies ran while one was open for 1% -> 0% of each run, Pallas kernels for 1% -> 1%
where the time goes in v3:
time: 84.5 us; the launch traced here: 84.1 us
  blocking collectives  58.1 us (69%)
  starting transfers between devices  11.9 us (14%)
  Pallas kernels  9.85 us (12%)
  waiting for transfers between devices  3.51 us (4%)
    all_to_all x3, blocking collectives, exchange(): return lax.all_to_all(pieces, axis, split_axis=0, concat_axis=0, tiled=True)  58.1 us
    pallas_call x6, Pallas kernels, call(): pl.pallas_call(body, in_specs=specs, out_specs=[spec for _, _, spec in ou...  9.85 us
    all_to_all x1, starting transfers between devices, exchange(): return lax.all_to_all(pieces, axis, split_axis=0, concat_axis=0, tiled=True)  6.69 us
    ppermute x1, starting transfers between devices, on_device(): other = lax.ppermute(spectrum, 'dp', [(0, 1), (1, 0)])  5.18 us
    ppermute x1, waiting for transfers between devices, on_device(): other = lax.ppermute(spectrum, 'dp', [(0, 1), (1, 0)])  3.5 us
  transfers between devices with their start and end apart: 2, of which 1 were waited for; matrix products, arithmetic and copies ran while one was open for 0% of the time, Pallas kernels for 1%

profile of v3, /device:TPU:1, one launch (start us, length us, event | category | flops | bytes accessed | tf_op | source)
XLA Modules:
  0.0 84.1 jit_solution(3993257035909500456)
XLA Ops:
  0.6 5.2 %shard_map.95 = (bf16[128,4096]{1,0:T(8,128)(2,1)S(1)}, bf16[8,128,256]{2,1,0:T(8,128)(2,1)S(1)}) custom-call(bf16[128,4096]{1,0:T(8,128)(2,1)} %bitcast.5, bf16[128,4096]{1,0:T(8,128)(2,1)} %bitcast.6, bf16[128,4096]{1,0:T(8,128)(2,1)} %bitcast.7, bf16[256,512]{1,0:T(8,128)(2,1)} %constant.6.clone.z_source.z_table, ...), custom_call_target="tpu_custom_call" | custom-call | tf_op jit(solution)/shard_map/pallas_call | solution.py:280
  5.8 0.0 copy-start
  5.8 23.7 %all_to_all.20.arrived = bf16[8,128,256]{2,1,0:T(8,128)(2,1)S(1)} all-to-all(bf16[8,128,256]{2,1,0:T(8,128)(2,1)S(1)} %get-tuple-element.6), channel_id=1, replica_groups=mesh['dp'=2,'gx'=32,'gy'=8] {'gy'}, dimensions={0} | all-to-all | bytes 1048576 | tf_op jit(solution)/shard_map/all_to_all | solution.py:291
  29.5 0.0 copy-done
  29.5 0.4 shard_map.96
  29.9 0.0 copy-start.3
  29.9 19.4 %all_to_all.21.arrived = bf16[32,32,128]{2,1,0:T(8,128)(2,1)S(1)} all-to-all(bf16[32,32,128]{2,1,0:T(8,128)(2,1)S(1)} %shard_map.96), channel_id=1, replica_groups=mesh['dp'=2,'gx'=32,'gy'=8] {'gx'}, dimensions={0} | all-to-all | bytes 524288 | tf_op jit(solution)/shard_map/all_to_all | solution.py:291
  49.3 0.0 copy-done.3
  49.3 0.5 shard_map.97
  49.8 15.1 %all_to_all.22.arrived = bf16[32,16,128]{2,1,0:T(8,128)(2,1)S(1)} all-to-all(bf16[32,16,128]{2,1,0:T(8,128)(2,1)S(1)} %get-tuple-element.7), channel_id=1, replica_groups=mesh['dp'=2,'gx'=32,'gy'=8] {'gx'}, dimensions={0} | all-to-all | bytes 262144 | tf_op jit(solution)/shard_map/all_to_all | solution.py:291
  64.9 0.0 copy-start.2
  64.9 1.1 %shard_map.98 = bf16[8,128,128]{2,1,0:T(8,128)(2,1)} custom-call(bf16[32,16,128]{2,1,0:T(8,128)(2,1)S(1)} %all_to_all.22.arrived, bf16[32,2,32,128]{3,2,1,0:T(8,128)(2,1)S(1)} %copy-done), custom_call_target="tpu_custom_call" | custom-call | tf_op jit(solution)/shard_map/pallas_call | solution.py:280
  65.9 0.0 copy-start.1
  65.9 6.7 %all-to-all-start.3 = ((bf16[8,128,128]{2,1,0:T(8,128)(2,1)}), bf16[8,128,128]{2,1,0:T(8,128)(2,1)S(1)}, u32[]{:S(2)}, u32[]{:S(2)}) async-start(bf16[8,128,128]{2,1,0:T(8,128)(2,1)} %shard_map.98), calls=%async_computation.3 | async-start | bytes 524288 | tf_op jit(solution)/shard_map/all_to_all | solution.py:291
  72.6 5.2 %collective-permute-start = (bf16[32,128]{1,0:T(8,128)(2,1)S(1)}, bf16[32,128]{1,0:T(8,128)(2,1)S(1)}, u32[]{:S(2)}, u32[]{:S(2)}) collective-permute-start(bf16[32,128]{1,0:T(8,128)(2,1)S(1)} %get-tuple-element.9.own), channel_id=1, source_target_pairs={{0,256},{256,0},{1,257},{257,1},{2,258},{258,2},{3,259},{259,3},{4... | collective-permute-start | bytes 24584 | tf_op jit(solution)/shard_map/ppermute | solution.py:341
  77.8 3.5 %collective-permute-done.other = bf16[32,128]{1,0:T(8,128)(2,1)S(1)} collective-permute-done((bf16[32,128]{1,0:T(8,128)(2,1)S(1)}, bf16[32,128]{1,0:T(8,128)(2,1)S(1)}, u32[]{:S(2)}, u32[]{:S(2)}) %collective-permute-start) | collective-permute-done | bytes 8224 | tf_op jit(solution)/shard_map/ppermute | solution.py:341
  81.3 0.0 copy-start.4
  81.3 0.9 %shard_map.100 = f32[2,1,32,2,256]{4,3,2,1,0:T(2,128)} custom-call(bf16[32,128]{1,0:T(8,128)(2,1)S(1)} %get-tuple-element.9.own, bf16[32,128]{1,0:T(8,128)(2,1)S(1)} %collective-permute-done.other), custom_call_target="tpu_custom_call" | custom-call | tf_op jit(solution)/shard_map/pallas_call | solution.py:280
  82.3 0.0 all-to-all-done.3.arrived
  82.3 0.0 copy-done.2
  82.3 0.0 copy-done.1
  82.3 0.0 copy-done.4
  82.3 1.8 %shard_map.99 = bf16[128,4096]{1,0:T(8,128)(2,1)} custom-call(bf16[8,128,128]{2,1,0:T(8,128)(2,1)S(1)} %all-to-all-done.3.arrived, bf16[128,4096]{1,0:T(8,128)(2,1)S(1)} %get-tuple-element.8.grad_pre, bf16[256,512]{1,0:T(8,128)(2,1)S(1)} %copy-done.2, bf16[8,128,256]{2,1,0:T(8,128)(2,1)S(1)} %copy-done.1, bf16[16,16]{1,0:T(8,128)(2,1)S(1)} %copy-done.4), custom_call_target="tpu_custom_call" | custom-call | tf_op jit(solution)/shard_map/pallas_call | solution.py:280
Async XLA Ops:
  5.8 23.7 %copy-start = (bf16[32,2,32,128]{3,2,1,0:T(8,128)(2,1)S(1)}, bf16[32,2,32,128]{3,2,1,0:T(8,128)(2,1)}, u32[]{:S(2)}) copy-start(bf16[32,2,32,128]{3,2,1,0:T(8,128)(2,1)} %constant.8.clone.x_rows) | copy-start | bytes 1572868
  29.9 19.4 %copy-start.3 = (bf16[2,1,32,2,256]{4,3,2,1,0:T(2,128)(2,1)S(1)}, bf16[2,1,32,2,256]{4,3,2,1,0:T(2,128)(2,1)}, u32[]{:S(2)}) copy-start(bf16[2,1,32,2,256]{4,3,2,1,0:T(2,128)(2,1)} %weights.1) | copy-start | bytes 196612
  64.9 17.4 %copy-start.2 = (bf16[256,512]{1,0:T(8,128)(2,1)S(1)}, bf16[256,512]{1,0:T(8,128)(2,1)}, u32[]{:S(2)}) copy-start(bf16[256,512]{1,0:T(8,128)(2,1)} %constant.6.clone.z_source.z_table) | copy-start | bytes 786436
  65.9 16.3 %copy-start.1 = (bf16[8,128,256]{2,1,0:T(8,128)(2,1)S(1)}, bf16[8,128,256]{2,1,0:T(8,128)(2,1)}, u32[]{:S(2)}) copy-start(bf16[8,128,256]{2,1,0:T(8,128)(2,1)} %constant.7.clone.y_source.y_tables) | copy-start | bytes 1572868
  65.9 16.3 %all-to-all-start.3 = ((bf16[8,128,128]{2,1,0:T(8,128)(2,1)}), bf16[8,128,128]{2,1,0:T(8,128)(2,1)S(1)}, u32[]{:S(2)}, u32[]{:S(2)}) async-start(bf16[8,128,128]{2,1,0:T(8,128)(2,1)} %shard_map.98), calls=%async_computation.3 | async-start | bytes 524288 | tf_op jit(solution)/shard_map/all_to_all | solution.py:291
  72.6 8.7 %collective-permute-start = (bf16[32,128]{1,0:T(8,128)(2,1)S(1)}, bf16[32,128]{1,0:T(8,128)(2,1)S(1)}, u32[]{:S(2)}, u32[]{:S(2)}) collective-permute-start(bf16[32,128]{1,0:T(8,128)(2,1)S(1)} %get-tuple-element.9.own), channel_id=1, source_target_pairs={{0,256},{256,0},{1,257},{257,1},{2,258},{258,2},{3,259},{259,3},{4... | collective-permute-start | bytes 24584 | tf_op jit(solution)/shard_map/ppermute | solution.py:341
  81.3 0.9 %copy-start.4 = (bf16[16,16]{1,0:T(8,128)(2,1)S(1)}, bf16[16,16]{1,0:T(8,128)(2,1)}, u32[]{:S(2)}) copy-start(bf16[16,16]{1,0:T(8,128)(2,1)} %point.1) | copy-start | bytes 1540

commit v4 on v3

--- a/solution.py
+++ b/solution.py
@@ -70,15 +70,15 @@
     return cdf + value * jnp.exp(-0.5 * value * value) * (1.0 / math.sqrt(2.0 * math.pi))
 
 
-def copies_in(sources, targets, sems, groups):
-    width = targets[0].shape[1] // groups
+def copies_in(sources, targets, sems):
+    width = targets[0].shape[1] // sems.shape[1]
     copies = []
-    for group in range(groups):
-        lanes = pl.ds(group * width, width)
+    for chunk in range(sems.shape[1]):
+        lanes = pl.ds(chunk * width, width)
         copies.append(
             [
                 pltpu.make_async_copy(
-                    source.at[:, lanes], target.at[:, lanes], sems.at[index, group]
+                    source.at[:, lanes], target.at[:, lanes], sems.at[index, chunk]
                 )
                 for index, (source, target) in enumerate(zip(sources, targets))
             ]
@@ -87,28 +87,30 @@
 
 
 def forward_zy(
-    fields, pre_act, cotangent, z_source, y_source, grad_pre, pieces,
+    fields, pre_act, cotangent, z_source, y_source, grad_pre, kept, given,
     fields_in, pre_in, cotangent_in, z_table, y_table, lines, sems, table_sems,
 ):
-    groups = sems.shape[1]
+    groups = pre_act.shape[1] // z_source.shape[1]
+    per_chunk = groups // sems.shape[1]
     tables = [
         pltpu.make_async_copy(z_source, z_table, table_sems.at[0]),
         pltpu.make_async_copy(y_source.at[lax.axis_index("gy")], y_table, table_sems.at[1]),
     ]
     copies = copies_in(
-        (pre_act, cotangent, fields), (pre_in, cotangent_in, fields_in), sems, groups
+        (pre_act, cotangent, fields), (pre_in, cotangent_in, fields_in), sems
     )
     for copy in copies[0] + tables[:1]:
         copy.start()
-    for group in copies[1:]:
-        for copy in group:
+    for chunk in copies[1:]:
+        for copy in chunk:
             copy.start()
     tables[1].start()
     width = pre_in.shape[1] // groups
     pair = []
-    for group, arrived in enumerate(copies):
-        for copy in arrived:
-            copy.wait()
+    for group in range(groups):
+        if group % per_chunk == 0:
+            for copy in copies[group // per_chunk]:
+                copy.wait()
         part = slice(group * width, (group + 1) * width)
         slope = gelu_slope(pre_in[:, part].astype(F32))
         grad = (cotangent_in[:, part].astype(F32) * slope).astype(BF16)
@@ -123,12 +125,22 @@
             lines[:, rows, :] = jnp.concatenate(pair, axis=1).astype(BF16)
             pair = []
     tables[1].wait()
-    count = pieces.shape[0]
+    side = lax.axis_index("gy") % 2
+    count = 2 * kept.shape[0]
     per = 2 * MZ // count
-    for index in range(count):
-        block = lines[index * per : (index + 1) * per]
-        block = block.reshape(per * block.shape[1], block.shape[2])
-        pieces[index] = dot(y_table[...], block, ((1,), (0,))).astype(BF16)
+    for index in range(count // 2):
+        for pieces, offset in ((given, 1 - side), (kept, side)):
+            first = (2 * index + offset) * per
+            block = lines[pl.ds(first, per)]
+            block = block.reshape(per * block.shape[1], block.shape[2])
+            pieces[index] = dot(y_table[...], block, ((1,), (0,))).astype(BF16)
+
+
+def add_halves(kept, taken, *sums):
+    chip = lax.axis_index("gy") // 2
+    for distance, total in enumerate(sums):
+        index = lax.rem(chip + distance, len(sums))
+        total[...] = (kept[index].astype(F32) + taken[index].astype(F32)).astype(BF16)
 
 
 def add_up(arrived):
@@ -150,9 +162,12 @@
     return blocks
 
 
-def forward_x(arrived, x_rows, pieces):
+def forward_x(*refs):
+    lines, x_rows, pieces = refs[:-2], refs[-2], refs[-1]
     blocks = x_blocks(x_rows)
-    total = add_up(arrived)
+    total = lines[0][...].astype(F32)
+    for term in lines[1:]:
+        total = total + term[...].astype(F32)
     half = total.shape[0] // 2
     swapped = jnp.concatenate([total[half:], -total[:half]], axis=0).astype(BF16)
     total = total.astype(BF16)
@@ -287,69 +302,32 @@
     )(*values)
 
 
-def exchange(pieces, axis):
-    return lax.all_to_all(pieces, axis, split_axis=0, concat_axis=0, tiled=True)
-
-
-def on_device(fields, pre_act, cotangent, spec_weight, point_weight):
-    count_x = lax.axis_size("gx")
-    count_y = lax.axis_size("gy")
-    _, channels, local_x, local_yz = fields.shape
+def run_forward_zy(fields, pre_act, cotangent, z_table, y_table, local_mz):
+    rows, local_yz = fields.shape
     local_y = local_yz // NZ
-    local_mz = spec_weight.shape[3]
-    rows = channels * local_x
     modes = MY * local_mz
-    groups = local_y // GROUP
-    z_table = jnp.asarray(z_block_table())
-    y_table = jnp.asarray(y_block_tables(count_y, local_y, local_mz))
-    x_rows = jnp.asarray(x_row_tables(count_x, local_x))
+    half = (MZ // local_mz // 2, 2 * modes, 2 * rows)
     whole = (rows, local_yz)
     dma = pltpu.SemaphoreType.DMA
-
-    grad_pre, pieces = call(
+    return call(
         forward_zy,
-        [
-            (fields.reshape(whole), HBM),
-            (pre_act.reshape(whole), HBM),
-            (cotangent.reshape(whole), HBM),
-            (z_table, HBM),
-            (y_table, HBM),
-        ],
-        [(whole, BF16, VMEM), ((count_y, 2 * modes, 2 * rows), BF16, VMEM)],
+        [(fields, HBM), (pre_act, HBM), (cotangent, HBM), (z_table, HBM), (y_table, HBM)],
+        [(whole, BF16, VMEM), (half, BF16, VMEM), (half, BF16, VMEM)],
         [pltpu.VMEM(whole, BF16)] * 3
         + [
             pltpu.VMEM(z_table.shape, BF16),
             pltpu.VMEM(y_table.shape[1:], BF16),
             pltpu.VMEM((2 * MZ, local_y, 2 * rows), BF16),
-            dma((3, groups)),
+            dma((3, 2)),
             dma((2,)),
         ],
     )
-    arrived = exchange(pieces, "gy")
-    (pieces,) = call(
-        forward_x,
-        [(arrived, VMEM), (x_rows, VMEM)],
-        [((count_x, 2 * C, 2 * modes), BF16, VMEM)],
-    )
-    arrived = exchange(pieces, "gx")
-    spectrum, pieces = call(
-        mode_products,
-        [(arrived, VMEM), (spec_weight, VMEM)],
-        [((2 * C, 2 * modes), BF16, VMEM), ((count_x, C, 2 * modes), BF16, VMEM)],
-    )
-    arrived = exchange(pieces, "gx")
-    other = lax.ppermute(spectrum, "dp", [(0, 1), (1, 0)])
-    (grad_spec,) = call(
-        weight_grads,
-        [(spectrum, VMEM), (other, VMEM)],
-        [(spec_weight.shape, F32, pl.BlockSpec())],
-    )
-    (pieces,) = call(
-        inverse_x,
-        [(arrived, VMEM), (x_rows, VMEM)],
-        [((count_y, 2 * modes, rows), BF16, VMEM)],
-    )
-    arrived = exchange(pieces, "gy")
+
+
+def run_inverse_yz(arrived, grad_pre, z_table, y_table, point_weight):
+    rows, local_yz = grad_pre.shape
+    local_y = local_yz // NZ
+    groups = local_y // GROUP
     (grad_fields,) = call(
         inverse_yz,
         [
@@ -359,13 +337,77 @@
             (y_table, VMEM),
             (point_weight, VMEM),
         ],
-        [(whole, BF16, HBM)],
+        [((rows, local_yz), BF16, HBM)],
         [
             pltpu.VMEM((2 * MZ, local_y, rows), F32),
-            pltpu.VMEM(whole, BF16),
-            dma((groups,)),
+            pltpu.VMEM((rows, local_yz), BF16),
+            pltpu.SemaphoreType.DMA((groups,)),
         ],
     )
+    return grad_fields
+
+
+def exchange(pieces, axis):
+    return lax.all_to_all(pieces, axis, split_axis=0, concat_axis=0, tiled=True)
+
+
+def on_device(fields, pre_act, cotangent, spec_weight, point_weight):
+    count_x = lax.axis_size("gx")
+    count_y = lax.axis_size("gy")
+    _, channels, local_x, local_yz = fields.shape
+    local_y = local_yz // NZ
+    local_mz = spec_weight.shape[3]
+    rows = channels * local_x
+    modes = MY * local_mz
+    z_table = jnp.asarray(z_block_table())
+    y_table = jnp.asarray(y_block_tables(count_y, local_y, local_mz))
+    x_rows = jnp.asarray(x_row_tables(count_x, local_x))
+    whole = (rows, local_yz)
+
+    grad_pre, kept, given = run_forward_zy(
+        fields.reshape(whole),
+        pre_act.reshape(whole),
+        cotangent.reshape(whole),
+        z_table,
+        y_table,
+        local_mz,
+    )
+    taken = lax.ppermute(given, "gy", [(i, i ^ 1) for i in range(count_y)])
+    chips = count_y // 2
+    lines = call(
+        add_halves,
+        [(kept, VMEM), (taken, VMEM)],
+        [((2 * modes, 2 * rows), BF16, VMEM)] * chips,
+    )
+    lines = [lines[0]] + [
+        lax.ppermute(lines[k], "gy", [(i, (i + 2 * k) % count_y) for i in range(count_y)])
+        for k in range(1, chips)
+    ]
+    (pieces,) = call(
+        forward_x,
+        [(line, VMEM) for line in lines] + [(x_rows, VMEM)],
+        [((count_x, 2 * C, 2 * modes), BF16, VMEM)],
+    )
+    arrived = exchange(pieces, "gx")
+    spectrum, pieces = call(
+        mode_products,
+        [(arrived, VMEM), (spec_weight, VMEM)],
+        [((2 * C, 2 * modes), BF16, VMEM), ((count_x, C, 2 * modes), BF16, VMEM)],
+    )
+    arrived = exchange(pieces, "gx")
+    other = lax.ppermute(spectrum, "dp", [(0, 1), (1, 0)])
+    (grad_spec,) = call(
+        weight_grads,
+        [(spectrum, VMEM), (other, VMEM)],
+        [(spec_weight.shape, F32, pl.BlockSpec())],
+    )
+    (pieces,) = call(
+        inverse_x,
+        [(arrived, VMEM), (x_rows, VMEM)],
+        [((count_y, 2 * modes, rows), BF16, VMEM)],
+    )
+    arrived = exchange(pieces, "gy")
+    grad_fields = run_inverse_yz(arrived, grad_pre, z_table, y_table, point_weight)
     return grad_fields.reshape(fields.shape), grad_spec
 
 

time: 84.5 us -> 81.3 us (0.962)
  blocking collectives: 58.1 us -> 32 us
  starting transfers between devices: 11.9 us -> 33.2 us
  waiting for transfers between devices: 3.51 us -> 6.72 us
  Pallas kernels: 9.85 us -> 8.11 us
    all_to_all x3 -> x2, blocking collectives: 58.1 us -> 32 us  [exchange(): return lax.all_to_all(pieces, axis, split_axis=0, concat_axis=0, tiled=True)]
    ppermute x0 -> x4, starting transfers between devices: none -> 17.9 us  [the longest x3 9 us: on_device(): lax.ppermute(lines[k], 'gy', [(i, (i + 2 * k) % count_y) for i in range(c...]
    ppermute x0 -> x4, waiting for transfers between devices: none -> 3.26 us  [the longest x3 2.12 us: on_device(): lax.ppermute(lines[k], 'gy', [(i, (i + 2 * k) % count_y) for i in range(c...]
    all_to_all x1, starting transfers between devices: 6.69 us -> 9.18 us  [exchange(): return lax.all_to_all(pieces, axis, split_axis=0, concat_axis=0, tiled=True)]
    pallas_call x6 -> x7, Pallas kernels: 9.85 us -> 8.11 us  [call(): pl.pallas_call(body, in_specs=specs, out_specs=[spec for _, _, spec in ou...]
    ppermute x1, starting transfers between devices: 5.18 us -> 6.1 us  [on_device(): other = lax.ppermute(spectrum, 'dp', [(0, 1), (1, 0)])]
  transfers between devices with their start and end apart: 2 -> 6, of which waited for: 1 -> 4; matrix products, arithmetic and copies ran while one was open for 0% -> 0% of each run, Pallas kernels for 1% -> 1%
where the time goes in v4:
time: 81.3 us; the launch traced here: 80.8 us
  starting transfers between devices  33.2 us (41%)
  blocking collectives  32 us (39%)
  Pallas kernels  8.11 us (10%)
  waiting for transfers between devices  6.72 us (8%)
    all_to_all x2, blocking collectives, exchange(): return lax.all_to_all(pieces, axis, split_axis=0, concat_axis=0, tiled=True)  32 us
    all_to_all x1, starting transfers between devices, exchange(): return lax.all_to_all(pieces, axis, split_axis=0, concat_axis=0, tiled=True)  9.18 us
    ppermute x3, starting transfers between devices, on_device(): lax.ppermute(lines[k], 'gy', [(i, (i + 2 * k) % count_y) for i in range(c...  9 us
    ppermute x1, starting transfers between devices, on_device(): taken = lax.ppermute(given, 'gy', [(i, i ^ 1) for i in range(count_y)])  8.88 us
    pallas_call x7, Pallas kernels, call(): pl.pallas_call(body, in_specs=specs, out_specs=[spec for _, _, spec in ou...  8.11 us
    ppermute x1, starting transfers between devices, on_device(): other = lax.ppermute(spectrum, 'dp', [(0, 1), (1, 0)])  6.1 us
    ppermute x1, waiting for transfers between devices, on_device(): other = lax.ppermute(spectrum, 'dp', [(0, 1), (1, 0)])  3.45 us
    ppermute x3, waiting for transfers between devices, on_device(): lax.ppermute(lines[k], 'gy', [(i, (i + 2 * k) % count_y) for i in range(c...  2.12 us
  transfers between devices with their start and end apart: 6, of which 4 were waited for; matrix products, arithmetic and copies ran while one was open for 0% of the time, Pallas kernels for 1%

profile of v4, /device:TPU:1, one launch (start us, length us, event | category | flops | bytes accessed | tf_op | source)
XLA Modules:
  0.0 80.8 jit_solution(4321201257495683728)
XLA Ops:
  0.6 3.4 %shard_map.95 = (bf16[128,4096]{1,0:T(8,128)(2,1)S(1)}, bf16[4,128,256]{2,1,0:T(8,128)(2,1)S(1)}, bf16[4,128,256]{2,1,0:T(8,128)(2,1)S(1)}) custom-call(bf16[128,4096]{1,0:T(8,128)(2,1)} %bitcast.5, bf16[128,4096]{1,0:T(8,128)(2,1)} %bitcast.6, bf16[128,4096]{1,0:T(8,128)(2,1)} %bitcast.7, bf16[256,512]{1,0:T(8,128)(2,1)} %constant.6.clone.z_source.z_table, ...), custom_call_target="tpu_custom_call" | custom-call | tf_op jit(solution)/shard_map/pallas_call | solution.py:295
  4.1 0.0 copy-start
  4.1 8.9 %collective-permute-start = (bf16[4,128,256]{2,1,0:T(8,128)(2,1)S(1)}, bf16[4,128,256]{2,1,0:T(8,128)(2,1)S(1)}, u32[]{:S(2)}, u32[]{:S(2)}) collective-permute-start(bf16[4,128,256]{2,1,0:T(8,128)(2,1)S(1)} %get-tuple-element.12), channel_id=1, source_target_pairs={{0,1},{1,0},{2,3},{3,2},{4,5},{5,4},{6,7},{7,6},{8,9},{9,8},{10,11... | collective-permute-start | bytes 786440 | tf_op jit(solution)/shard_map/ppermute | solution.py:375
  13.0 1.1 %collective-permute-done.taken = bf16[4,128,256]{2,1,0:T(8,128)(2,1)S(1)} collective-permute-done((bf16[4,128,256]{2,1,0:T(8,128)(2,1)S(1)}, bf16[4,128,256]{2,1,0:T(8,128)(2,1)S(1)}, u32[]{:S(2)}, u32[]{:S(2)}) %collective-permute-start) | collective-permute-done | bytes 262176 | tf_op jit(solution)/shard_map/ppermute | solution.py:375
  14.1 0.1 shard_map.96
  14.2 1.9 %collective-permute-start.1 = (bf16[128,256]{1,0:T(8,128)(2,1)S(1)}, bf16[128,256]{1,0:T(8,128)(2,1)S(1)}, u32[]{:S(2)}, u32[]{:S(2)}) collective-permute-start(bf16[128,256]{1,0:T(8,128)(2,1)S(1)} %get-tuple-element.14), channel_id=1, source_target_pairs={{0,2},{1,3},{2,4},{3,5},{4,6},{5,7},{6,0},{7,1},{8,10},{9,11},{10,... | collective-permute-start | bytes 196616 | tf_op jit(solution)/shard_map/ppermute | solution.py:383
  16.1 1.9 %collective-permute-start.2 = (bf16[128,256]{1,0:T(8,128)(2,1)S(1)}, bf16[128,256]{1,0:T(8,128)(2,1)S(1)}, u32[]{:S(2)}, u32[]{:S(2)}) collective-permute-start(bf16[128,256]{1,0:T(8,128)(2,1)S(1)} %get-tuple-element.15), channel_id=1, source_target_pairs={{0,4},{1,5},{2,6},{3,7},{4,0},{5,1},{6,2},{7,3},{8,12},{9,13},{10,... | collective-permute-start | bytes 196616 | tf_op jit(solution)/shard_map/ppermute | solution.py:383
  18.0 5.2 %collective-permute-start.3 = (bf16[128,256]{1,0:T(8,128)(2,1)S(1)}, bf16[128,256]{1,0:T(8,128)(2,1)S(1)}, u32[]{:S(2)}, u32[]{:S(2)}) collective-permute-start(bf16[128,256]{1,0:T(8,128)(2,1)S(1)} %get-tuple-element.16), channel_id=1, source_target_pairs={{0,6},{1,7},{2,0},{3,1},{4,2},{5,3},{6,4},{7,5},{8,14},{9,15},{10,... | collective-permute-start | bytes 196616 | tf_op jit(solution)/shard_map/ppermute | solution.py:383
  23.2 0.0 collective-permute-done.1.refs_1_
  23.2 1.4 %collective-permute-done.2.refs_2_ = bf16[128,256]{1,0:T(8,128)(2,1)S(1)} collective-permute-done((bf16[128,256]{1,0:T(8,128)(2,1)S(1)}, bf16[128,256]{1,0:T(8,128)(2,1)S(1)}, u32[]{:S(2)}, u32[]{:S(2)}) %collective-permute-start.2) | collective-permute-done | bytes 65568 | tf_op jit(solution)/shard_map/ppermute | solution.py:383
  24.6 0.7 collective-permute-done.3.refs_3_
  25.3 0.0 copy-done
  25.3 0.3 shard_map.97
  25.6 0.0 copy-start.3
  25.7 18.4 %all_to_all.15.arrived = bf16[32,32,128]{2,1,0:T(8,128)(2,1)S(1)} all-to-all(bf16[32,32,128]{2,1,0:T(8,128)(2,1)S(1)} %shard_map.97), channel_id=1, replica_groups=mesh['dp'=2,'gx'=32,'gy'=8] {'gx'}, dimensions={0} | all-to-all | bytes 524288 | tf_op jit(solution)/shard_map/all_to_all | solution.py:351
  44.1 0.0 copy-done.3
  44.1 0.5 shard_map.98
  44.6 13.6 %all_to_all.16.arrived = bf16[32,16,128]{2,1,0:T(8,128)(2,1)S(1)} all-to-all(bf16[32,16,128]{2,1,0:T(8,128)(2,1)S(1)} %get-tuple-element.17), channel_id=1, replica_groups=mesh['dp'=2,'gx'=32,'gy'=8] {'gx'}, dimensions={0} | all-to-all | bytes 262144 | tf_op jit(solution)/shard_map/all_to_all | solution.py:351
  58.2 0.0 copy-start.2
  58.2 1.1 %shard_map.99 = bf16[8,128,128]{2,1,0:T(8,128)(2,1)} custom-call(bf16[32,16,128]{2,1,0:T(8,128)(2,1)S(1)} %all_to_all.16.arrived, bf16[32,2,32,128]{3,2,1,0:T(8,128)(2,1)S(1)} %copy-done), custom_call_target="tpu_custom_call" | custom-call | tf_op jit(solution)/shard_map/pallas_call | solution.py:295
  59.3 0.0 copy-start.1
  59.3 9.2 %all-to-all-start.2 = ((bf16[8,128,128]{2,1,0:T(8,128)(2,1)}), bf16[8,128,128]{2,1,0:T(8,128)(2,1)S(1)}, u32[]{:S(2)}, u32[]{:S(2)}) async-start(bf16[8,128,128]{2,1,0:T(8,128)(2,1)} %shard_map.99), calls=%async_computation.2 | async-start | bytes 524288 | tf_op jit(solution)/shard_map/all_to_all | solution.py:351
  68.5 6.1 %collective-permute-start.4 = (bf16[32,128]{1,0:T(8,128)(2,1)S(1)}, bf16[32,128]{1,0:T(8,128)(2,1)S(1)}, u32[]{:S(2)}, u32[]{:S(2)}) collective-permute-start(bf16[32,128]{1,0:T(8,128)(2,1)S(1)} %get-tuple-element.19.own), channel_id=1, source_target_pairs={{0,256},{256,0},{1,257},{257,1},{2,258},{258,2},{3,259},{259,3},{4... | collective-permute-start | bytes 24584 | tf_op jit(solution)/shard_map/ppermute | solution.py:398
  74.6 3.5 %collective-permute-done.4.other = bf16[32,128]{1,0:T(8,128)(2,1)S(1)} collective-permute-done((bf16[32,128]{1,0:T(8,128)(2,1)S(1)}, bf16[32,128]{1,0:T(8,128)(2,1)S(1)}, u32[]{:S(2)}, u32[]{:S(2)}) %collective-permute-start.4) | collective-permute-done | bytes 8224 | tf_op jit(solution)/shard_map/ppermute | solution.py:398
  78.0 0.0 copy-start.4
  78.0 0.9 %shard_map.101 = f32[2,1,32,2,256]{4,3,2,1,0:T(2,128)} custom-call(bf16[32,128]{1,0:T(8,128)(2,1)S(1)} %get-tuple-element.19.own, bf16[32,128]{1,0:T(8,128)(2,1)S(1)} %collective-permute-done.4.other), custom_call_target="tpu_custom_call" | custom-call | tf_op jit(solution)/shard_map/pallas_call | solution.py:295
  79.0 0.0 all-to-all-done.2.arrived
  79.0 0.0 copy-done.2
  79.0 0.0 copy-done.1
  79.0 0.0 copy-done.4
  79.0 1.8 %shard_map.100 = bf16[128,4096]{1,0:T(8,128)(2,1)} custom-call(bf16[8,128,128]{2,1,0:T(8,128)(2,1)S(1)} %all-to-all-done.2.arrived, bf16[128,4096]{1,0:T(8,128)(2,1)S(1)} %get-tuple-element.18.grad_pre, bf16[256,512]{1,0:T(8,128)(2,1)S(1)} %copy-done.2, bf16[8,128,256]{2,1,0:T(8,128)(2,1)S(1)} %copy-done.1, bf16[16,16]{1,0:T(8,128)(2,1)S(1)} %copy-done.4), custom_call_target="tpu_custom_call" | custom-call | tf_op jit(solution)/shard_map/pallas_call | solution.py:295
Async XLA Ops:
  4.1 21.3 %copy-start = (bf16[32,2,32,128]{3,2,1,0:T(8,128)(2,1)S(1)}, bf16[32,2,32,128]{3,2,1,0:T(8,128)(2,1)}, u32[]{:S(2)}) copy-start(bf16[32,2,32,128]{3,2,1,0:T(8,128)(2,1)} %constant.8.clone.refs_4_.x_rows) | copy-start | bytes 1572868
  4.1 10.0 %collective-permute-start = (bf16[4,128,256]{2,1,0:T(8,128)(2,1)S(1)}, bf16[4,128,256]{2,1,0:T(8,128)(2,1)S(1)}, u32[]{:S(2)}, u32[]{:S(2)}) collective-permute-start(bf16[4,128,256]{2,1,0:T(8,128)(2,1)S(1)} %get-tuple-element.12), channel_id=1, source_target_pairs={{0,1},{1,0},{2,3},{3,2},{4,5},{5,4},{6,7},{7,6},{8,9},{9,8},{10,11... | collective-permute-start | bytes 786440 | tf_op jit(solution)/shard_map/ppermute | solution.py:375
  14.2 9.0 %collective-permute-start.1 = (bf16[128,256]{1,0:T(8,128)(2,1)S(1)}, bf16[128,256]{1,0:T(8,128)(2,1)S(1)}, u32[]{:S(2)}, u32[]{:S(2)}) collective-permute-start(bf16[128,256]{1,0:T(8,128)(2,1)S(1)} %get-tuple-element.14), channel_id=1, source_target_pairs={{0,2},{1,3},{2,4},{3,5},{4,6},{5,7},{6,0},{7,1},{8,10},{9,11},{10,... | collective-permute-start | bytes 196616 | tf_op jit(solution)/shard_map/ppermute | solution.py:383
  16.1 8.5 %collective-permute-start.2 = (bf16[128,256]{1,0:T(8,128)(2,1)S(1)}, bf16[128,256]{1,0:T(8,128)(2,1)S(1)}, u32[]{:S(2)}, u32[]{:S(2)}) collective-permute-start(bf16[128,256]{1,0:T(8,128)(2,1)S(1)} %get-tuple-element.15), channel_id=1, source_target_pairs={{0,4},{1,5},{2,6},{3,7},{4,0},{5,1},{6,2},{7,3},{8,12},{9,13},{10,... | collective-permute-start | bytes 196616 | tf_op jit(solution)/shard_map/ppermute | solution.py:383
  18.0 7.3 %collective-permute-start.3 = (bf16[128,256]{1,0:T(8,128)(2,1)S(1)}, bf16[128,256]{1,0:T(8,128)(2,1)S(1)}, u32[]{:S(2)}, u32[]{:S(2)}) collective-permute-start(bf16[128,256]{1,0:T(8,128)(2,1)S(1)} %get-tuple-element.16), channel_id=1, source_target_pairs={{0,6},{1,7},{2,0},{3,1},{4,2},{5,3},{6,4},{7,5},{8,14},{9,15},{10,... | collective-permute-start | bytes 196616 | tf_op jit(solution)/shard_map/ppermute | solution.py:383
  25.6 18.4 %copy-start.3 = (bf16[2,1,32,2,256]{4,3,2,1,0:T(2,128)(2,1)S(1)}, bf16[2,1,32,2,256]{4,3,2,1,0:T(2,128)(2,1)}, u32[]{:S(2)}) copy-start(bf16[2,1,32,2,256]{4,3,2,1,0:T(2,128)(2,1)} %weights.1) | copy-start | bytes 196612
  58.2 20.8 %copy-start.2 = (bf16[256,512]{1,0:T(8,128)(2,1)S(1)}, bf16[256,512]{1,0:T(8,128)(2,1)}, u32[]{:S(2)}) copy-start(bf16[256,512]{1,0:T(8,128)(2,1)} %constant.6.clone.z_source.z_table) | copy-start | bytes 786436
  59.3 19.7 %copy-start.1 = (bf16[8,128,256]{2,1,0:T(8,128)(2,1)S(1)}, bf16[8,128,256]{2,1,0:T(8,128)(2,1)}, u32[]{:S(2)}) copy-start(bf16[8,128,256]{2,1,0:T(8,128)(2,1)} %constant.7.clone.y_source.y_tables) | copy-start | bytes 1572868
  59.3 19.7 %all-to-all-start.2 = ((bf16[8,128,128]{2,1,0:T(8,128)(2,1)}), bf16[8,128,128]{2,1,0:T(8,128)(2,1)S(1)}, u32[]{:S(2)}, u32[]{:S(2)}) async-start(bf16[8,128,128]{2,1,0:T(8,128)(2,1)} %shard_map.99), calls=%async_computation.2 | async-start | bytes 524288 | tf_op jit(solution)/shard_map/all_to_all | solution.py:351
  68.5 9.6 %collective-permute-start.4 = (bf16[32,128]{1,0:T(8,128)(2,1)S(1)}, bf16[32,128]{1,0:T(8,128)(2,1)S(1)}, u32[]{:S(2)}, u32[]{:S(2)}) collective-permute-start(bf16[32,128]{1,0:T(8,128)(2,1)S(1)} %get-tuple-element.19.own), channel_id=1, source_target_pairs={{0,256},{256,0},{1,257},{257,1},{2,258},{258,2},{3,259},{259,3},{4... | collective-permute-start | bytes 24584 | tf_op jit(solution)/shard_map/ppermute | solution.py:398
  78.0 0.9 %copy-start.4 = (bf16[16,16]{1,0:T(8,128)(2,1)S(1)}, bf16[16,16]{1,0:T(8,128)(2,1)}, u32[]{:S(2)}) copy-start(bf16[16,16]{1,0:T(8,128)(2,1)} %point.1) | copy-start | bytes 1540

commit v5 on v4

--- a/solution.py
+++ b/solution.py
@@ -1,3 +1,4 @@
+import functools
 import math
 
 import jax
@@ -136,11 +137,19 @@
             pieces[index] = dot(y_table[...], block, ((1,), (0,))).astype(BF16)
 
 
-def add_halves(kept, taken, *sums):
-    chip = lax.axis_index("gy") // 2
-    for distance, total in enumerate(sums):
-        index = lax.rem(chip + distance, len(sums))
-        total[...] = (kept[index].astype(F32) + taken[index].astype(F32)).astype(BF16)
+def add_halves(bit, kept, taken, keep, give):
+    side = lax.axis_index("gy") // bit % 2
+    for index in range(keep.shape[0]):
+        for total, offset in ((give, 1 - side), (keep, side)):
+            place = 2 * index + offset
+            total[index] = (kept[place].astype(F32) + taken[place].astype(F32)).astype(BF16)
+
+
+def join_halves(bit, own, taken, joined):
+    side = lax.axis_index("gy") // bit % 2
+    for index in range(own.shape[0]):
+        joined[2 * index + side] = own[index]
+        joined[2 * index + 1 - side] = taken[index]
 
 
 def add_up(arrived):
@@ -162,12 +171,9 @@
     return blocks
 
 
-def forward_x(*refs):
-    lines, x_rows, pieces = refs[:-2], refs[-2], refs[-1]
+def forward_x(kept, taken, x_rows, pieces):
     blocks = x_blocks(x_rows)
-    total = lines[0][...].astype(F32)
-    for term in lines[1:]:
-        total = total + term[...].astype(F32)
+    total = kept[0].astype(F32) + taken[0].astype(F32)
     half = total.shape[0] // 2
     swapped = jnp.concatenate([total[half:], -total[:half]], axis=0).astype(BF16)
     total = total.astype(BF16)
@@ -238,11 +244,11 @@
     half = values.shape[1] // 2
     swapped = jnp.concatenate([-values[:, half:], values[:, :half]], axis=1)
     sums = dot(values, blocks[0], ((0,), (0,))) + dot(swapped, blocks[1], ((0,), (0,)))
-    result[...] = jnp.broadcast_to(sums.astype(BF16)[None], result.shape)
+    result[0] = sums.astype(BF16)
 
 
 def inverse_yz(
-    arrived, grad_pre, z_table, y_tables, point, result, lines, staged, sems
+    own, taken, grad_pre, z_table, y_tables, point, result, lines, staged, sems
 ):
     y_table = y_tables[lax.axis_index("gy")]
     rows = staged.shape[0]
@@ -254,11 +260,13 @@
     left = lax.broadcasted_iota(jnp.int32, (rows, rows), 0) % local_x
     right = lax.broadcasted_iota(jnp.int32, (rows, rows), 1) % local_x
     mixing = jnp.where(left == right, spread, 0.0).astype(BF16)
-    count = arrived.shape[0]
-    per = 2 * MZ // count
-    for index in range(count):
-        block = dot(y_table, arrived[index], ((0,), (0,)))
-        lines[index * per : (index + 1) * per] = block.reshape(per, -1, rows)
+    side = lax.axis_index("gy") % 2
+    per = MZ // own.shape[0]
+    for index in range(own.shape[0]):
+        for spectra, offset in ((own, side), (taken, 1 - side)):
+            block = dot(y_table, spectra[index], ((0,), (0,)))
+            first = (2 * index + offset) * per
+            lines[pl.ds(first, per)] = block.reshape(per, -1, rows)
     width = z_table.shape[1]
     copies = []
     for group in range(result.shape[1] // width):
@@ -324,14 +332,15 @@
     )
 
 
-def run_inverse_yz(arrived, grad_pre, z_table, y_table, point_weight):
+def run_inverse_yz(own, taken, grad_pre, z_table, y_table, point_weight):
     rows, local_yz = grad_pre.shape
     local_y = local_yz // NZ
     groups = local_y // GROUP
     (grad_fields,) = call(
         inverse_yz,
         [
-            (arrived, VMEM),
+            (own, VMEM),
+            (taken, VMEM),
             (grad_pre, VMEM),
             (z_table, VMEM),
             (y_table, VMEM),
@@ -345,6 +354,10 @@
         ],
     )
     return grad_fields
+
+
+def swap(values, axis, bit):
+    return lax.ppermute(values, axis, [(i, i ^ bit) for i in range(lax.axis_size(axis))])
 
 
 def exchange(pieces, axis):
@@ -372,20 +385,18 @@
         y_table,
         local_mz,
     )
-    taken = lax.ppermute(given, "gy", [(i, i ^ 1) for i in range(count_y)])
-    chips = count_y // 2
-    lines = call(
-        add_halves,
-        [(kept, VMEM), (taken, VMEM)],
-        [((2 * modes, 2 * rows), BF16, VMEM)] * chips,
-    )
-    lines = [lines[0]] + [
-        lax.ppermute(lines[k], "gy", [(i, (i + 2 * k) % count_y) for i in range(count_y)])
-        for k in range(1, chips)
-    ]
+    taken = swap(given, "gy", 1)
+    for bit in (2, 4):
+        half = ((kept.shape[0] // 2,) + kept.shape[1:], BF16, VMEM)
+        kept, given = call(
+            functools.partial(add_halves, bit),
+            [(kept, VMEM), (taken, VMEM)],
+            [half, half],
+        )
+        taken = swap(given, "gy", bit)
     (pieces,) = call(
         forward_x,
-        [(line, VMEM) for line in lines] + [(x_rows, VMEM)],
+        [(kept, VMEM), (taken, VMEM), (x_rows, VMEM)],
         [((count_x, 2 * C, 2 * modes), BF16, VMEM)],
     )
     arrived = exchange(pieces, "gx")
@@ -395,7 +406,7 @@
         [((2 * C, 2 * modes), BF16, VMEM), ((count_x, C, 2 * modes), BF16, VMEM)],
     )
     arrived = exchange(pieces, "gx")
-    other = lax.ppermute(spectrum, "dp", [(0, 1), (1, 0)])
+    other = swap(spectrum, "dp", 1)
     (grad_spec,) = call(
         weight_grads,
         [(spectrum, VMEM), (other, VMEM)],
@@ -404,10 +415,17 @@
     (pieces,) = call(
         inverse_x,
         [(arrived, VMEM), (x_rows, VMEM)],
-        [((count_y, 2 * modes, rows), BF16, VMEM)],
-    )
-    arrived = exchange(pieces, "gy")
-    grad_fields = run_inverse_yz(arrived, grad_pre, z_table, y_table, point_weight)
+        [((1, 2 * modes, rows), BF16, VMEM)],
+    )
+    taken = swap(pieces, "gy", 4)
+    for bit in (4, 2):
+        (pieces,) = call(
+            functools.partial(join_halves, bit),
+            [(pieces, VMEM), (taken, VMEM)],
+            [((2 * pieces.shape[0],) + pieces.shape[1:], BF16, VMEM)],
+        )
+        taken = swap(pieces, "gy", bit // 2)
+    grad_fields = run_inverse_yz(pieces, taken, grad_pre, z_table, y_table, point_weight)
     return grad_fields.reshape(fields.shape), grad_spec
 
 

time: 81.3 us -> 91.1 us (1.12)
  waiting for transfers between devices: 6.72 us -> 14.8 us
  starting transfers between devices: 33.2 us -> 37.5 us
  blocking collectives: 32 us -> 30 us
    ppermute x5 -> x7, starting transfers between devices: 24 us -> 37.5 us  [swap(): lax.ppermute(values, axis, [(i, i ^ bit) for i in range(lax.axis_size(axi...]
    all_to_all x1 -> x0, starting transfers between devices: 9.18 us -> none  [exchange(): return lax.all_to_all(pieces, axis, split_axis=0, concat_axis=0, tiled=True)]
    ppermute x5 -> x7, waiting for transfers between devices: 6.71 us -> 14.8 us  [swap(): lax.ppermute(values, axis, [(i, i ^ bit) for i in range(lax.axis_size(axi...]
    all_to_all x2, blocking collectives: 32 us -> 30 us  [exchange(): return lax.all_to_all(pieces, axis, split_axis=0, concat_axis=0, tiled=True)]
    pallas_call x7 -> x10, Pallas kernels: 8.11 us -> 7.53 us  [call(): pl.pallas_call(body, in_specs=specs, out_specs=[spec for _, _, spec in ou...]
  transfers between devices with their start and end apart: 6 -> 7, of which waited for: 4 -> 6; matrix products, arithmetic and copies ran while one was open for 0% -> 0% of each run, Pallas kernels for 1% -> 1%
where the time goes in v5:
time: 91.1 us; the launch traced here: 90.6 us
  starting transfers between devices  37.5 us (41%)
  blocking collectives  30 us (33%)
  waiting for transfers between devices  14.8 us (16%)
  Pallas kernels  7.53 us (8%)
    ppermute x7, starting transfers between devices, swap(): lax.ppermute(values, axis, [(i, i ^ bit) for i in range(lax.axis_size(axi...  37.5 us
    all_to_all x2, blocking collectives, exchange(): return lax.all_to_all(pieces, axis, split_axis=0, concat_axis=0, tiled=True)  30 us
    ppermute x7, waiting for transfers between devices, swap(): lax.ppermute(values, axis, [(i, i ^ bit) for i in range(lax.axis_size(axi...  14.8 us
    pallas_call x10, Pallas kernels, call(): pl.pallas_call(body, in_specs=specs, out_specs=[spec for _, _, spec in ou...  7.53 us
  transfers between devices with their start and end apart: 7, of which 6 were waited for; matrix products, arithmetic and copies ran while one was open for 0% of the time, Pallas kernels for 1%

profile of v5, /device:TPU:1, one launch (start us, length us, event | category | flops | bytes accessed | tf_op | source)
XLA Modules:
  0.0 90.6 jit_solution(3629488922606013007)
XLA Ops:
  0.6 3.4 %shard_map.95 = (bf16[128,4096]{1,0:T(8,128)(2,1)S(1)}, bf16[4,128,256]{2,1,0:T(8,128)(2,1)S(1)}, bf16[4,128,256]{2,1,0:T(8,128)(2,1)S(1)}) custom-call(bf16[128,4096]{1,0:T(8,128)(2,1)} %bitcast.5, bf16[128,4096]{1,0:T(8,128)(2,1)} %bitcast.6, bf16[128,4096]{1,0:T(8,128)(2,1)} %bitcast.7, bf16[256,512]{1,0:T(8,128)(2,1)} %constant.6.clone.z_source.z_table, ...), custom_call_target="tpu_custom_call" | custom-call | tf_op jit(solution)/shard_map/pallas_call | solution.py:303
  4.1 0.0 copy-start
  4.1 8.9 %collective-permute-start = (bf16[4,128,256]{2,1,0:T(8,128)(2,1)S(1)}, bf16[4,128,256]{2,1,0:T(8,128)(2,1)S(1)}, u32[]{:S(2)}, u32[]{:S(2)}) collective-permute-start(bf16[4,128,256]{2,1,0:T(8,128)(2,1)S(1)} %get-tuple-element.12), channel_id=1, source_target_pairs={{0,1},{1,0},{2,3},{3,2},{4,5},{5,4},{6,7},{7,6},{8,9},{9,8},{10,11... | collective-permute-start | bytes 786440 | tf_op jit(solution)/shard_map/ppermute | solution.py:360
  13.0 1.1 %collective-permute-done.taken = bf16[4,128,256]{2,1,0:T(8,128)(2,1)S(1)} collective-permute-done((bf16[4,128,256]{2,1,0:T(8,128)(2,1)S(1)}, bf16[4,128,256]{2,1,0:T(8,128)(2,1)S(1)}, u32[]{:S(2)}, u32[]{:S(2)}) %collective-permute-start) | collective-permute-done | bytes 262176 | tf_op jit(solution)/shard_map/ppermute | solution.py:360
  14.1 0.1 shard_map.96
  14.2 1.9 %collective-permute-start.1 = (bf16[2,128,256]{2,1,0:T(8,128)(2,1)S(1)}, bf16[2,128,256]{2,1,0:T(8,128)(2,1)S(1)}, u32[]{:S(2)}, u32[]{:S(2)}) collective-permute-start(bf16[2,128,256]{2,1,0:T(8,128)(2,1)S(1)} %get-tuple-element.14), channel_id=1, source_target_pairs={{0,2},{1,3},{2,0},{3,1},{4,6},{5,7},{6,4},{7,5},{8,10},{9,11},{10,... | collective-permute-start | bytes 393224 | tf_op jit(solution)/shard_map/ppermute | solution.py:360
  16.1 4.6 %collective-permute-done.1.taken = bf16[2,128,256]{2,1,0:T(8,128)(2,1)S(1)} collective-permute-done((bf16[2,128,256]{2,1,0:T(8,128)(2,1)S(1)}, bf16[2,128,256]{2,1,0:T(8,128)(2,1)S(1)}, u32[]{:S(2)}, u32[]{:S(2)}) %collective-permute-start.1) | collective-permute-done | bytes 131104 | tf_op jit(solution)/shard_map/ppermute | solution.py:360
  20.8 1.9 %collective-permute-start.2 = (bf16[1,128,256]{2,1,0:T(8,128)(2,1)S(1)}, bf16[1,128,256]{2,1,0:T(8,128)(2,1)S(1)}, u32[]{:S(2)}, u32[]{:S(2)}) collective-permute-start(bf16[1,128,256]{2,1,0:T(8,128)(2,1)S(1)} %get-tuple-element.16), channel_id=1, source_target_pairs={{0,4},{1,5},{2,6},{3,7},{4,0},{5,1},{6,2},{7,3},{8,12},{9,13},{10,... | collective-permute-start | bytes 196616 | tf_op jit(solution)/shard_map/ppermute | solution.py:360
  22.7 4.7 %collective-permute-done.2.taken = bf16[1,128,256]{2,1,0:T(8,128)(2,1)S(1)} collective-permute-done((bf16[1,128,256]{2,1,0:T(8,128)(2,1)S(1)}, bf16[1,128,256]{2,1,0:T(8,128)(2,1)S(1)}, u32[]{:S(2)}, u32[]{:S(2)}) %collective-permute-start.2) | collective-permute-done | bytes 65568 | tf_op jit(solution)/shard_map/ppermute | solution.py:360
  27.4 0.0 copy-done
  27.4 0.3 shard_map.98
  27.7 0.0 copy-start.3
  27.7 16.4 %all_to_all.10.arrived = bf16[32,32,128]{2,1,0:T(8,128)(2,1)S(1)} all-to-all(bf16[32,32,128]{2,1,0:T(8,128)(2,1)S(1)} %shard_map.98), channel_id=1, replica_groups=mesh['dp'=2,'gx'=32,'gy'=8] {'gx'}, dimensions={0} | all-to-all | bytes 524288 | tf_op jit(solution)/shard_map/all_to_all | solution.py:364
  44.1 0.0 copy-done.3
  44.1 0.5 shard_map.99
  44.7 13.6 %all_to_all.11.arrived = bf16[32,16,128]{2,1,0:T(8,128)(2,1)S(1)} all-to-all(bf16[32,16,128]{2,1,0:T(8,128)(2,1)S(1)} %get-tuple-element.17), channel_id=1, replica_groups=mesh['dp'=2,'gx'=32,'gy'=8] {'gx'}, dimensions={0} | all-to-all | bytes 262144 | tf_op jit(solution)/shard_map/all_to_all | solution.py:364
  58.3 0.0 copy-start.1
  58.3 0.4 shard_map.100.own
  58.7 0.0 copy-start.2
  58.7 4.4 %collective-permute-start.3 = (bf16[1,128,128]{2,1,0:T(8,128)(2,1)S(1)}, bf16[1,128,128]{2,1,0:T(8,128)(2,1)S(1)}, u32[]{:S(2)}, u32[]{:S(2)}) collective-permute-start(bf16[1,128,128]{2,1,0:T(8,128)(2,1)S(1)} %shard_map.100.own), channel_id=1, source_target_pairs={{0,4},{1,5},{2,6},{3,7},{4,0},{5,1},{6,2},{7,3},{8,12},{9,13},{10,... | collective-permute-start | bytes 98312 | tf_op jit(solution)/shard_map/ppermute | solution.py:360
  63.1 1.3 %collective-permute-done.3.taken = bf16[1,128,128]{2,1,0:T(8,128)(2,1)S(1)} collective-permute-done((bf16[1,128,128]{2,1,0:T(8,128)(2,1)S(1)}, bf16[1,128,128]{2,1,0:T(8,128)(2,1)S(1)}, u32[]{:S(2)}, u32[]{:S(2)}) %collective-permute-start.3) | collective-permute-done | bytes 32800 | tf_op jit(solution)/shard_map/ppermute | solution.py:360
  64.4 3.7 %collective-permute-start.4 = (bf16[2,128,128]{2,1,0:T(8,128)(2,1)S(1)}, bf16[2,128,128]{2,1,0:T(8,128)(2,1)S(1)}, u32[]{:S(2)}, u32[]{:S(2)}) collective-permute-start(bf16[2,128,128]{2,1,0:T(8,128)(2,1)S(1)} %shard_map.101.own), channel_id=1, source_target_pairs={{0,2},{1,3},{2,0},{3,1},{4,6},{5,7},{6,4},{7,5},{8,10},{9,11},{10,... | collective-permute-start | bytes 196616 | tf_op jit(solution)/shard_map/ppermute | solution.py:360
  68.1 2.0 %collective-permute-done.4.taken = bf16[2,128,128]{2,1,0:T(8,128)(2,1)S(1)} collective-permute-done((bf16[2,128,128]{2,1,0:T(8,128)(2,1)S(1)}, bf16[2,128,128]{2,1,0:T(8,128)(2,1)S(1)}, u32[]{:S(2)}, u32[]{:S(2)}) %collective-permute-start.4) | collective-permute-done | bytes 65568 | tf_op jit(solution)/shard_map/ppermute | solution.py:360
  70.1 8.5 %collective-permute-start.5 = (bf16[4,128,128]{2,1,0:T(8,128)(2,1)S(1)}, bf16[4,128,128]{2,1,0:T(8,128)(2,1)S(1)}, u32[]{:S(2)}, u32[]{:S(2)}) collective-permute-start(bf16[4,128,128]{2,1,0:T(8,128)(2,1)S(1)} %shard_map.102.own), channel_id=1, source_target_pairs={{0,1},{1,0},{2,3},{3,2},{4,5},{5,4},{6,7},{7,6},{8,9},{9,8},{10,11... | collective-permute-start | bytes 393224 | tf_op jit(solution)/shard_map/ppermute | solution.py:360
  78.7 8.1 %collective-permute-start.6 = (bf16[32,128]{1,0:T(8,128)(2,1)S(1)}, bf16[32,128]{1,0:T(8,128)(2,1)S(1)}, u32[]{:S(2)}, u32[]{:S(2)}) collective-permute-start(bf16[32,128]{1,0:T(8,128)(2,1)S(1)} %get-tuple-element.19.own), channel_id=1, source_target_pairs={{0,256},{256,0},{1,257},{257,1},{2,258},{258,2},{3,259},{259,3},{4... | collective-permute-start | bytes 24584 | tf_op jit(solution)/shard_map/ppermute | solution.py:360
  86.8 1.0 %collective-permute-done.6.other = bf16[32,128]{1,0:T(8,128)(2,1)S(1)} collective-permute-done((bf16[32,128]{1,0:T(8,128)(2,1)S(1)}, bf16[32,128]{1,0:T(8,128)(2,1)S(1)}, u32[]{:S(2)}, u32[]{:S(2)}) %collective-permute-start.6) | collective-permute-done | bytes 8224 | tf_op jit(solution)/shard_map/ppermute | solution.py:360
  87.8 0.0 copy-start.4
  87.8 0.9 %shard_map.104 = f32[2,1,32,2,256]{4,3,2,1,0:T(2,128)} custom-call(bf16[32,128]{1,0:T(8,128)(2,1)S(1)} %get-tuple-element.19.own, bf16[32,128]{1,0:T(8,128)(2,1)S(1)} %collective-permute-done.6.other), custom_call_target="tpu_custom_call" | custom-call | tf_op jit(solution)/shard_map/pallas_call | solution.py:303
  88.7 0.0 collective-permute-done.5.taken
  88.7 0.0 copy-done.1
  88.7 0.0 copy-done.2
  88.8 0.0 copy-done.4
  88.8 1.9 %shard_map.103 = bf16[128,4096]{1,0:T(8,128)(2,1)} custom-call(bf16[4,128,128]{2,1,0:T(8,128)(2,1)S(1)} %shard_map.102.own, bf16[4,128,128]{2,1,0:T(8,128)(2,1)S(1)} %collective-permute-done.5.taken, bf16[128,4096]{1,0:T(8,128)(2,1)S(1)} %get-tuple-element.18.grad_pre, bf16[256,512]{1,0:T(8,128)(2,1)S(1)} %copy-done.2, bf16[8,128,256]{2,1,0:T(8,128)(2,1)S(1)} %copy-done.1, ...), custom_call_target="tpu_custom_call" | custom-call | tf_op jit(solution)/shard_map/pallas_call | solution.py:303
  (3 shorter events, 0.1 us)
Async XLA Ops:
  4.1 23.3 %copy-start = (bf16[32,2,32,128]{3,2,1,0:T(8,128)(2,1)S(1)}, bf16[32,2,32,128]{3,2,1,0:T(8,128)(2,1)}, u32[]{:S(2)}) copy-start(bf16[32,2,32,128]{3,2,1,0:T(8,128)(2,1)} %constant.8.clone.x_rows) | copy-start | bytes 1572868
  4.1 10.0 %collective-permute-start = (bf16[4,128,256]{2,1,0:T(8,128)(2,1)S(1)}, bf16[4,128,256]{2,1,0:T(8,128)(2,1)S(1)}, u32[]{:S(2)}, u32[]{:S(2)}) collective-permute-start(bf16[4,128,256]{2,1,0:T(8,128)(2,1)S(1)} %get-tuple-element.12), channel_id=1, source_target_pairs={{0,1},{1,0},{2,3},{3,2},{4,5},{5,4},{6,7},{7,6},{8,9},{9,8},{10,11... | collective-permute-start | bytes 786440 | tf_op jit(solution)/shard_map/ppermute | solution.py:360
  14.2 6.6 %collective-permute-start.1 = (bf16[2,128,256]{2,1,0:T(8,128)(2,1)S(1)}, bf16[2,128,256]{2,1,0:T(8,128)(2,1)S(1)}, u32[]{:S(2)}, u32[]{:S(2)}) collective-permute-start(bf16[2,128,256]{2,1,0:T(8,128)(2,1)S(1)} %get-tuple-element.14), channel_id=1, source_target_pairs={{0,2},{1,3},{2,0},{3,1},{4,6},{5,7},{6,4},{7,5},{8,10},{9,11},{10,... | collective-permute-start | bytes 393224 | tf_op jit(solution)/shard_map/ppermute | solution.py:360
  20.8 6.6 %collective-permute-start.2 = (bf16[1,128,256]{2,1,0:T(8,128)(2,1)S(1)}, bf16[1,128,256]{2,1,0:T(8,128)(2,1)S(1)}, u32[]{:S(2)}, u32[]{:S(2)}) collective-permute-start(bf16[1,128,256]{2,1,0:T(8,128)(2,1)S(1)} %get-tuple-element.16), channel_id=1, source_target_pairs={{0,4},{1,5},{2,6},{3,7},{4,0},{5,1},{6,2},{7,3},{8,12},{9,13},{10,... | collective-permute-start | bytes 196616 | tf_op jit(solution)/shard_map/ppermute | solution.py:360
  27.7 16.4 %copy-start.3 = (bf16[2,1,32,2,256]{4,3,2,1,0:T(2,128)(2,1)S(1)}, bf16[2,1,32,2,256]{4,3,2,1,0:T(2,128)(2,1)}, u32[]{:S(2)}) copy-start(bf16[2,1,32,2,256]{4,3,2,1,0:T(2,128)(2,1)} %weights.1) | copy-start | bytes 196612
  58.3 30.5 %copy-start.1 = (bf16[8,128,256]{2,1,0:T(8,128)(2,1)S(1)}, bf16[8,128,256]{2,1,0:T(8,128)(2,1)}, u32[]{:S(2)}) copy-start(bf16[8,128,256]{2,1,0:T(8,128)(2,1)} %constant.7.clone.y_source.y_tables) | copy-start | bytes 1572868
  58.7 30.1 %copy-start.2 = (bf16[256,512]{1,0:T(8,128)(2,1)S(1)}, bf16[256,512]{1,0:T(8,128)(2,1)}, u32[]{:S(2)}) copy-start(bf16[256,512]{1,0:T(8,128)(2,1)} %constant.6.clone.z_source.z_table) | copy-start | bytes 786436
  58.7 5.7 %collective-permute-start.3 = (bf16[1,128,128]{2,1,0:T(8,128)(2,1)S(1)}, bf16[1,128,128]{2,1,0:T(8,128)(2,1)S(1)}, u32[]{:S(2)}, u32[]{:S(2)}) collective-permute-start(bf16[1,128,128]{2,1,0:T(8,128)(2,1)S(1)} %shard_map.100.own), channel_id=1, source_target_pairs={{0,4},{1,5},{2,6},{3,7},{4,0},{5,1},{6,2},{7,3},{8,12},{9,13},{10,... | collective-permute-start | bytes 98312 | tf_op jit(solution)/shard_map/ppermute | solution.py:360
  64.4 5.7 %collective-permute-start.4 = (bf16[2,128,128]{2,1,0:T(8,128)(2,1)S(1)}, bf16[2,128,128]{2,1,0:T(8,128)(2,1)S(1)}, u32[]{:S(2)}, u32[]{:S(2)}) collective-permute-start(bf16[2,128,128]{2,1,0:T(8,128)(2,1)S(1)} %shard_map.101.own), channel_id=1, source_target_pairs={{0,2},{1,3},{2,0},{3,1},{4,6},{5,7},{6,4},{7,5},{8,10},{9,11},{10,... | collective-permute-start | bytes 196616 | tf_op jit(solution)/shard_map/ppermute | solution.py:360
  70.1 18.6 %collective-permute-start.5 = (bf16[4,128,128]{2,1,0:T(8,128)(2,1)S(1)}, bf16[4,128,128]{2,1,0:T(8,128)(2,1)S(1)}, u32[]{:S(2)}, u32[]{:S(2)}) collective-permute-start(bf16[4,128,128]{2,1,0:T(8,128)(2,1)S(1)} %shard_map.102.own), channel_id=1, source_target_pairs={{0,1},{1,0},{2,3},{3,2},{4,5},{5,4},{6,7},{7,6},{8,9},{9,8},{10,11... | collective-permute-start | bytes 393224 | tf_op jit(solution)/shard_map/ppermute | solution.py:360
  78.7 9.1 %collective-permute-start.6 = (bf16[32,128]{1,0:T(8,128)(2,1)S(1)}, bf16[32,128]{1,0:T(8,128)(2,1)S(1)}, u32[]{:S(2)}, u32[]{:S(2)}) collective-permute-start(bf16[32,128]{1,0:T(8,128)(2,1)S(1)} %get-tuple-element.19.own), channel_id=1, source_target_pairs={{0,256},{256,0},{1,257},{257,1},{2,258},{258,2},{3,259},{259,3},{4... | collective-permute-start | bytes 24584 | tf_op jit(solution)/shard_map/ppermute | solution.py:360
  87.8 0.9 %copy-start.4 = (bf16[16,16]{1,0:T(8,128)(2,1)S(1)}, bf16[16,16]{1,0:T(8,128)(2,1)}, u32[]{:S(2)}) copy-start(bf16[16,16]{1,0:T(8,128)(2,1)} %point.1) | copy-start | bytes 1540

commit v6 on v4

--- a/solution.py
+++ b/solution.py
@@ -19,7 +19,6 @@
 
 F32 = jnp.float32
 BF16 = jnp.bfloat16
-HIGHEST = lax.Precision.HIGHEST
 
 
 def signed_freqs(kept, length):
@@ -59,10 +58,8 @@
     return np.tile(table, (1, 1, 1, 128 // local_x)).astype(BF16)
 
 
-def dot(left, right, dims, precision=None):
-    return lax.dot_general(
-        left, right, (dims, ((), ())), preferred_element_type=F32, precision=precision
-    )
+def dot(left, right, dims):
+    return lax.dot_general(left, right, (dims, ((), ())), preferred_element_type=F32)
 
 
 def gelu_slope(value):
@@ -136,11 +133,8 @@
             pieces[index] = dot(y_table[...], block, ((1,), (0,))).astype(BF16)
 
 
-def add_halves(kept, taken, *sums):
-    chip = lax.axis_index("gy") // 2
-    for distance, total in enumerate(sums):
-        index = lax.rem(chip + distance, len(sums))
-        total[...] = (kept[index].astype(F32) + taken[index].astype(F32)).astype(BF16)
+def add_halves(kept, taken, sums):
+    sums[...] = (kept[...].astype(F32) + taken[...].astype(F32)).astype(BF16)
 
 
 def add_up(arrived):
@@ -162,12 +156,9 @@
     return blocks
 
 
-def forward_x(*refs):
-    lines, x_rows, pieces = refs[:-2], refs[-2], refs[-1]
+def forward_x(arrived, x_rows, pieces):
     blocks = x_blocks(x_rows)
-    total = lines[0][...].astype(F32)
-    for term in lines[1:]:
-        total = total + term[...].astype(F32)
+    total = add_up(arrived)
     half = total.shape[0] // 2
     swapped = jnp.concatenate([total[half:], -total[:half]], axis=0).astype(BF16)
     total = total.astype(BF16)
@@ -208,7 +199,13 @@
     products = jnp.concatenate(
         [real_w * real_d + imag_w * imag_d, real_w * imag_d - imag_w * real_d], axis=0
     )
-    values = dot(outer, products, ((1,), (1,)), HIGHEST).astype(BF16)
+    values = None
+    for _ in range(3):
+        piece = products.astype(BF16)
+        products = products - piece.astype(F32)
+        term = dot(outer.astype(BF16), piece, ((1,), (1,)))
+        values = term if values is None else values + term
+    values = values.astype(BF16)
     grad_hat[...] = jnp.broadcast_to(values[None], grad_hat.shape)
 
 
@@ -347,8 +344,10 @@
     return grad_fields
 
 
-def exchange(pieces, axis):
-    return lax.all_to_all(pieces, axis, split_axis=0, concat_axis=0, tiled=True)
+def exchange(pieces, axis, groups=None):
+    return lax.all_to_all(
+        pieces, axis, split_axis=0, concat_axis=0, tiled=True, axis_index_groups=groups
+    )
 
 
 def on_device(fields, pre_act, cotangent, spec_weight, point_weight):
@@ -373,19 +372,12 @@
         local_mz,
     )
     taken = lax.ppermute(given, "gy", [(i, i ^ 1) for i in range(count_y)])
-    chips = count_y // 2
-    lines = call(
-        add_halves,
-        [(kept, VMEM), (taken, VMEM)],
-        [((2 * modes, 2 * rows), BF16, VMEM)] * chips,
-    )
-    lines = [lines[0]] + [
-        lax.ppermute(lines[k], "gy", [(i, (i + 2 * k) % count_y) for i in range(count_y)])
-        for k in range(1, chips)
-    ]
+    (sums,) = call(add_halves, [(kept, VMEM), (taken, VMEM)], [(kept.shape, BF16, VMEM)])
+    sides = [list(range(side, count_y, 2)) for side in range(2)]
+    arrived = exchange(sums, "gy", sides)
     (pieces,) = call(
         forward_x,
-        [(line, VMEM) for line in lines] + [(x_rows, VMEM)],
+        [(arrived, VMEM), (x_rows, VMEM)],
         [((count_x, 2 * C, 2 * modes), BF16, VMEM)],
     )
     arrived = exchange(pieces, "gx")

time: 81.3 us -> 79.7 us (0.980)
  blocking collectives: 32 us -> 42.3 us
  starting transfers between devices: 33.2 us -> 23.6 us
  waiting for transfers between devices: 6.72 us -> 4.65 us
    all_to_all x2 -> x3, blocking collectives: 32 us -> 42.3 us  [exchange(): lax.all_to_all(pieces, axis, split_axis=0, concat_axis=0, tiled=True, axi...]
    ppermute x3 -> x0, starting transfers between devices: 9 us -> none  [on_device(): lax.ppermute(lines[k], 'gy', [(i, (i + 2 * k) % count_y) for i in range(c...]
    ppermute x3 -> x0, waiting for transfers between devices: 2.12 us -> none  [on_device(): lax.ppermute(lines[k], 'gy', [(i, (i + 2 * k) % count_y) for i in range(c...]
  transfers between devices with their start and end apart: 6 -> 3, of which waited for: 4 -> 2; matrix products, arithmetic and copies ran while one was open for 0% -> 0% of each run, Pallas kernels for 1% -> 1%
where the time goes in v6:
time: 79.7 us; the launch traced here: 79.3 us
  blocking collectives  42.3 us (53%)
  starting transfers between devices  23.6 us (30%)
  Pallas kernels  8.08 us (10%)
  waiting for transfers between devices  4.65 us (6%)
    all_to_all x3, blocking collectives, exchange(): lax.all_to_all(pieces, axis, split_axis=0, concat_axis=0, tiled=True, axi...  42.3 us
    all_to_all x1, starting transfers between devices, exchange(): lax.all_to_all(pieces, axis, split_axis=0, concat_axis=0, tiled=True, axi...  9.24 us
    ppermute x1, starting transfers between devices, on_device(): taken = lax.ppermute(given, 'gy', [(i, i ^ 1) for i in range(count_y)])  8.75 us
    pallas_call x7, Pallas kernels, call(): pl.pallas_call(body, in_specs=specs, out_specs=[spec for _, _, spec in ou...  8.08 us
    ppermute x1, starting transfers between devices, on_device(): other = lax.ppermute(spectrum, 'dp', [(0, 1), (1, 0)])  5.58 us
    ppermute x1, waiting for transfers between devices, on_device(): other = lax.ppermute(spectrum, 'dp', [(0, 1), (1, 0)])  3.5 us
  transfers between devices with their start and end apart: 3, of which 2 were waited for; matrix products, arithmetic and copies ran while one was open for 0% of the time, Pallas kernels for 1%

profile of v6, /device:TPU:1, one launch (start us, length us, event | category | flops | bytes accessed | tf_op | source)
XLA Modules:
  0.0 79.3 jit_solution(10753147812914845241)
XLA Ops:
  0.6 3.4 %shard_map.95 = (bf16[128,4096]{1,0:T(8,128)(2,1)S(1)}, bf16[4,128,256]{2,1,0:T(8,128)(2,1)S(1)}, bf16[4,128,256]{2,1,0:T(8,128)(2,1)S(1)}) custom-call(bf16[128,4096]{1,0:T(8,128)(2,1)} %bitcast.5, bf16[128,4096]{1,0:T(8,128)(2,1)} %bitcast.6, bf16[128,4096]{1,0:T(8,128)(2,1)} %bitcast.7, bf16[256,512]{1,0:T(8,128)(2,1)} %constant.6.clone.z_source.z_table, ...), custom_call_target="tpu_custom_call" | custom-call | tf_op jit(solution)/shard_map/pallas_call | solution.py:292
  4.1 8.7 %collective-permute-start = (bf16[4,128,256]{2,1,0:T(8,128)(2,1)S(1)}, bf16[4,128,256]{2,1,0:T(8,128)(2,1)S(1)}, u32[]{:S(2)}, u32[]{:S(2)}) collective-permute-start(bf16[4,128,256]{2,1,0:T(8,128)(2,1)S(1)} %get-tuple-element.8), channel_id=1, source_target_pairs={{0,1},{1,0},{2,3},{3,2},{4,5},{5,4},{6,7},{7,6},{8,9},{9,8},{10,11... | collective-permute-start | bytes 786440 | tf_op jit(solution)/shard_map/ppermute | solution.py:374
  12.8 1.1 %collective-permute-done.taken = bf16[4,128,256]{2,1,0:T(8,128)(2,1)S(1)} collective-permute-done((bf16[4,128,256]{2,1,0:T(8,128)(2,1)S(1)}, bf16[4,128,256]{2,1,0:T(8,128)(2,1)S(1)}, u32[]{:S(2)}, u32[]{:S(2)}) %collective-permute-start) | collective-permute-done | bytes 262176 | tf_op jit(solution)/shard_map/ppermute | solution.py:374
  14.0 0.0 copy-start
  14.0 0.1 shard_map.96
  14.0 10.8 %all_to_all.20.arrived = bf16[4,128,256]{2,1,0:T(8,128)(2,1)S(1)} all-to-all(bf16[4,128,256]{2,1,0:T(8,128)(2,1)S(1)} %shard_map.96), channel_id=1, replica_groups={{0,2,4,6},{1,3,5,7},{8,10,12,14},{9,11,13,15},{16,18,20,22},{17,19,21,2..., dimensions={0} | all-to-all | bytes 524288 | tf_op jit(solution)/shard_map/all_to_all | solution.py:348
  24.8 0.0 copy-done
  24.8 0.3 shard_map.97
  25.1 0.0 copy-start.3
  25.1 18.0 %all_to_all.21.arrived = bf16[32,32,128]{2,1,0:T(8,128)(2,1)S(1)} all-to-all(bf16[32,32,128]{2,1,0:T(8,128)(2,1)S(1)} %shard_map.97), channel_id=1, replica_groups=mesh['dp'=2,'gx'=32,'gy'=8] {'gx'}, dimensions={0} | all-to-all | bytes 524288 | tf_op jit(solution)/shard_map/all_to_all | solution.py:348
  43.1 0.0 copy-done.3
  43.1 0.5 shard_map.98
  43.6 13.6 %all_to_all.22.arrived = bf16[32,16,128]{2,1,0:T(8,128)(2,1)S(1)} all-to-all(bf16[32,16,128]{2,1,0:T(8,128)(2,1)S(1)} %get-tuple-element.9), channel_id=1, replica_groups=mesh['dp'=2,'gx'=32,'gy'=8] {'gx'}, dimensions={0} | all-to-all | bytes 262144 | tf_op jit(solution)/shard_map/all_to_all | solution.py:348
  57.1 0.0 copy-start.2
  57.1 1.1 %shard_map.99 = bf16[8,128,128]{2,1,0:T(8,128)(2,1)} custom-call(bf16[32,16,128]{2,1,0:T(8,128)(2,1)S(1)} %all_to_all.22.arrived, bf16[32,2,32,128]{3,2,1,0:T(8,128)(2,1)S(1)} %copy-done), custom_call_target="tpu_custom_call" | custom-call | tf_op jit(solution)/shard_map/pallas_call | solution.py:292
  58.2 0.0 copy-start.1
  58.2 9.2 %all-to-all-start.3 = ((bf16[8,128,128]{2,1,0:T(8,128)(2,1)}), bf16[8,128,128]{2,1,0:T(8,128)(2,1)S(1)}, u32[]{:S(2)}, u32[]{:S(2)}) async-start(bf16[8,128,128]{2,1,0:T(8,128)(2,1)} %shard_map.99), calls=%async_computation.3 | async-start | bytes 524288 | tf_op jit(solution)/shard_map/all_to_all | solution.py:348
  67.5 5.6 %collective-permute-start.1 = (bf16[32,128]{1,0:T(8,128)(2,1)S(1)}, bf16[32,128]{1,0:T(8,128)(2,1)S(1)}, u32[]{:S(2)}, u32[]{:S(2)}) collective-permute-start(bf16[32,128]{1,0:T(8,128)(2,1)S(1)} %get-tuple-element.11.own), channel_id=1, source_target_pairs={{0,256},{256,0},{1,257},{257,1},{2,258},{258,2},{3,259},{259,3},{4... | collective-permute-start | bytes 24584 | tf_op jit(solution)/shard_map/ppermute | solution.py:390
  73.1 3.5 %collective-permute-done.1.other = bf16[32,128]{1,0:T(8,128)(2,1)S(1)} collective-permute-done((bf16[32,128]{1,0:T(8,128)(2,1)S(1)}, bf16[32,128]{1,0:T(8,128)(2,1)S(1)}, u32[]{:S(2)}, u32[]{:S(2)}) %collective-permute-start.1) | collective-permute-done | bytes 8224 | tf_op jit(solution)/shard_map/ppermute | solution.py:390
  76.6 0.0 copy-start.4
  76.6 0.9 %shard_map.101 = f32[2,1,32,2,256]{4,3,2,1,0:T(2,128)} custom-call(bf16[32,128]{1,0:T(8,128)(2,1)S(1)} %get-tuple-element.11.own, bf16[32,128]{1,0:T(8,128)(2,1)S(1)} %collective-permute-done.1.other), custom_call_target="tpu_custom_call" | custom-call | tf_op jit(solution)/shard_map/pallas_call | solution.py:292
  77.5 0.0 all-to-all-done.3.arrived
  77.5 0.0 copy-done.2
  77.5 0.0 copy-done.1
  77.5 0.0 copy-done.4
  77.5 1.8 %shard_map.100 = bf16[128,4096]{1,0:T(8,128)(2,1)} custom-call(bf16[8,128,128]{2,1,0:T(8,128)(2,1)S(1)} %all-to-all-done.3.arrived, bf16[128,4096]{1,0:T(8,128)(2,1)S(1)} %get-tuple-element.10.grad_pre, bf16[256,512]{1,0:T(8,128)(2,1)S(1)} %copy-done.2, bf16[8,128,256]{2,1,0:T(8,128)(2,1)S(1)} %copy-done.1, bf16[16,16]{1,0:T(8,128)(2,1)S(1)} %copy-done.4), custom_call_target="tpu_custom_call" | custom-call | tf_op jit(solution)/shard_map/pallas_call | solution.py:292
Async XLA Ops:
  4.1 9.9 %collective-permute-start = (bf16[4,128,256]{2,1,0:T(8,128)(2,1)S(1)}, bf16[4,128,256]{2,1,0:T(8,128)(2,1)S(1)}, u32[]{:S(2)}, u32[]{:S(2)}) collective-permute-start(bf16[4,128,256]{2,1,0:T(8,128)(2,1)S(1)} %get-tuple-element.8), channel_id=1, source_target_pairs={{0,1},{1,0},{2,3},{3,2},{4,5},{5,4},{6,7},{7,6},{8,9},{9,8},{10,11... | collective-permute-start | bytes 786440 | tf_op jit(solution)/shard_map/ppermute | solution.py:374
  14.0 10.8 %copy-start = (bf16[32,2,32,128]{3,2,1,0:T(8,128)(2,1)S(1)}, bf16[32,2,32,128]{3,2,1,0:T(8,128)(2,1)}, u32[]{:S(2)}) copy-start(bf16[32,2,32,128]{3,2,1,0:T(8,128)(2,1)} %constant.8.clone.x_rows) | copy-start | bytes 1572868
  25.1 18.0 %copy-start.3 = (bf16[2,1,32,2,256]{4,3,2,1,0:T(2,128)(2,1)S(1)}, bf16[2,1,32,2,256]{4,3,2,1,0:T(2,128)(2,1)}, u32[]{:S(2)}) copy-start(bf16[2,1,32,2,256]{4,3,2,1,0:T(2,128)(2,1)} %weights.1) | copy-start | bytes 196612
  57.1 20.4 %copy-start.2 = (bf16[256,512]{1,0:T(8,128)(2,1)S(1)}, bf16[256,512]{1,0:T(8,128)(2,1)}, u32[]{:S(2)}) copy-start(bf16[256,512]{1,0:T(8,128)(2,1)} %constant.6.clone.z_source.z_table) | copy-start | bytes 786436
  58.2 19.3 %copy-start.1 = (bf16[8,128,256]{2,1,0:T(8,128)(2,1)S(1)}, bf16[8,128,256]{2,1,0:T(8,128)(2,1)}, u32[]{:S(2)}) copy-start(bf16[8,128,256]{2,1,0:T(8,128)(2,1)} %constant.7.clone.y_source.y_tables) | copy-start | bytes 1572868
  58.2 19.3 %all-to-all-start.3 = ((bf16[8,128,128]{2,1,0:T(8,128)(2,1)}), bf16[8,128,128]{2,1,0:T(8,128)(2,1)S(1)}, u32[]{:S(2)}, u32[]{:S(2)}) async-start(bf16[8,128,128]{2,1,0:T(8,128)(2,1)} %shard_map.99), calls=%async_computation.3 | async-start | bytes 524288 | tf_op jit(solution)/shard_map/all_to_all | solution.py:348
  67.5 9.1 %collective-permute-start.1 = (bf16[32,128]{1,0:T(8,128)(2,1)S(1)}, bf16[32,128]{1,0:T(8,128)(2,1)S(1)}, u32[]{:S(2)}, u32[]{:S(2)}) collective-permute-start(bf16[32,128]{1,0:T(8,128)(2,1)S(1)} %get-tuple-element.11.own), channel_id=1, source_target_pairs={{0,256},{256,0},{1,257},{257,1},{2,258},{258,2},{3,259},{259,3},{4... | collective-permute-start | bytes 24584 | tf_op jit(solution)/shard_map/ppermute | solution.py:390
  76.6 0.9 %copy-start.4 = (bf16[16,16]{1,0:T(8,128)(2,1)S(1)}, bf16[16,16]{1,0:T(8,128)(2,1)}, u32[]{:S(2)}) copy-start(bf16[16,16]{1,0:T(8,128)(2,1)} %point.1) | copy-start | bytes 1540
